TPU v7x, 32 devices: a whole 2x2x4 slice. The times are simulated.
32 devices in a mesh: parts: 2 (over x), blk: 16 (over z, y, core).
Axes of the slice: x: 2, y: 2, z: 4, core: 2. Of those that a mesh axis runs over, the one named last changes fastest.
Arguments:
- particles: bfloat16 [256, 2, 2048], P(('parts', 'blk')), parts along dimension 0, may hold values from -56 to 56, as said below
- offsets: int32 [2, 256], P(None, ('parts', 'blk')), parts along dimension 1, may hold values from -2 to 2
- references: bfloat16 [128, 2, 2048], P(('parts', 'blk')), parts along dimension 0, may hold values from -4 to 4, as said below
- inv_noise: float32 [32], replicated, may hold values from 0.01 to 0.04
- counts: int32 [32], P('parts'), parts along dimension 0, may hold values from 1 to 8, 48 in all
Outputs:
- loglik: float32 [256], P(('parts', 'blk')), parts along dimension 0
- class_sums: float32 [128, 2, 2048], P(('parts', 'blk')), parts along dimension 0
There are 2 independent parts, one for each index of `parts`. A program takes and returns all parts, laid end to end along the dimension named above; an argument that names none is the same for every part. Nothing has to cross between parts.
Inputs may be any that keep to these rules, and one draw needn't show every extreme that they name: The particles of blk index d fill its first counts[d] slots; the counts sum to 48 and the largest is 8. `particles`: particle coefficients; slots beyond a device's count hold values that no output reads. `references`: class reference coefficients.
All inputs are finite; a program needn't handle non-finite values.
Results may differ from a plain program's by a relative error of at most 0.0075.
Values may be sent and summed in bfloat16 or wider, within the bound.
No kernel may reach another device: no remote copies, remote signals or barrier semaphores. Data moves between devices by JAX's collectives and lax.ppermute only.
A program may use at most 64 MiB of HBM per device.

v0:
```python
import functools
import math

import jax
import jax.numpy as jnp
import numpy as np
from jax import lax
from jax.experimental import pallas as pl
from jax.experimental.pallas import tpu as pltpu
from jax.sharding import PartitionSpec as P

ANGLES = 64
SHIFT = 5
STEPS = SHIFT * SHIFT
MEAN = 3
CHUNK = 48
ROWS = STEPS * CHUNK
PAIR = 4 * ANGLES
F32 = jnp.float32
BF16 = jnp.bfloat16
VMEM_LIMIT = 60 * 1024 * 1024


def split(table, terms):
    rest = np.asarray(table, np.float64)
    out = []
    for _ in range(terms):
        piece = rest.astype(np.float32).astype(jnp.bfloat16)
        out.append(piece)
        rest = rest - piece.astype(np.float64)
    return out


def angle_products():
    index = np.arange(ANGLES)
    radians = 2.0 * math.pi / ANGLES * (index[:, None] * index[None, :] % ANGLES)
    return np.cos(radians), np.sin(radians)


def step_phases(cycles):
    polar = 2.0 * math.pi / ANGLES * np.arange(ANGLES)
    radius = np.arange(1, cycles + 1)
    step = np.arange(STEPS)
    along = (step // SHIFT - SHIFT // 2)[:, None] * np.cos(polar) + (step % SHIFT - SHIFT // 2)[
        :, None
    ] * np.sin(polar)
    phases = 2.0 * math.pi / 128.0 * radius[None, :, None] * along[:, None, :]
    return np.cos(phases), np.sin(phases)


def step_tables(cycles):
    cosine, sine = step_phases(cycles)
    tc = np.concatenate([cosine, cosine], axis=2).reshape(STEPS, -1).astype(np.float32)
    ts = np.concatenate([sine, -sine], axis=2).reshape(STEPS, -1).astype(np.float32)
    return tc, ts


def offset_table(cycles):
    cosine, sine = step_phases(cycles)
    both = np.concatenate([cosine.reshape(STEPS, -1), sine.reshape(STEPS, -1)], axis=1)
    both = np.pad(both, ((0, 32 - STEPS), (0, 0)))
    return np.concatenate(split(both, 3), axis=0)


def forward_matrix():
    cosine, sine = angle_products()
    return np.block([[cosine, -sine], [sine, cosine]])


def forward_stack():
    high, low = split(forward_matrix(), 2)
    return np.block([[high, low], [high, np.zeros_like(low)]])


def rotation_tables():
    cosine, sine = angle_products()
    cosine, sine = cosine / ANGLES, sine / ANGLES
    return (
        np.concatenate([cosine, cosine], axis=1).astype(np.float32),
        np.concatenate([sine, -sine], axis=1).astype(np.float32),
    )


def gather_tables():
    cosine, sine = angle_products()
    return (
        np.concatenate([cosine] * 4, axis=1).astype(np.float32),
        np.concatenate([sine] * 4, axis=1).astype(np.float32),
    )


def image_stack():
    cosine, sine = angle_products()
    table = np.zeros((2, 2, ANGLES, 2, 2, ANGLES))
    for parity in range(2):
        table[parity, 0, :, 0, parity] = cosine / ANGLES
        table[parity, 1, :, 0, parity] = -sine / ANGLES
        table[parity, 0, :, 1, parity] = sine / ANGLES
        table[parity, 1, :, 1, parity] = cosine / ANGLES
    high, low = split(table.reshape(PAIR, PAIR), 2)
    return np.concatenate([high, low], axis=1)


def dot(left, right, dims=((1,), (0,))):
    return lax.dot_general(left, right, (dims, ((), ())), preferred_element_type=F32)


def halves(value):
    high = value.astype(BF16)
    return high, (value - high.astype(F32)).astype(BF16)


def spectra_kernel(cycles, noise_ref, refs_ref, trio_ref, cos_ref, sin_ref, bt_ref, hat_ref, swap_ref):
    classes = refs_ref.shape[0] // cycles
    raw = dot(refs_ref[...], trio_ref[...])
    hat = (raw[:, :128] + raw[:, 128:256]) + raw[:, 256:]
    hat_ref[...] = hat
    swap_ref[...] = pltpu.roll(hat, 64, 1)
    cosine, sine = cos_ref[...], sin_ref[...]
    columns = classes * ANGLES

    def body(j, carry):
        weight = noise_ref[j]
        lanes = pl.ds(pl.multiple_of(j * 128, 128), 128)
        for c in range(classes):
            row = pl.ds(c * cycles + j, 1)
            plain = (hat_ref[row, :] * weight).astype(BF16).astype(F32)
            swapped = (swap_ref[row, :] * weight).astype(BF16).astype(F32)
            high, low = halves(plain * cosine + swapped * sine)
            bt_ref[c * ANGLES : (c + 1) * ANGLES, lanes] = high
            bt_ref[columns + c * ANGLES : columns + (c + 1) * ANGLES, lanes] = low
        return carry

    lax.fori_loop(0, cycles, body, 0)


def rotated_spectra(references, inv_noise, cycles):
    classes = references.shape[0]
    refs = references.reshape(classes, 2, cycles, ANGLES).transpose(0, 2, 1, 3)
    refs = refs.reshape(classes * cycles, 2 * ANGLES)
    trio = np.concatenate(split(forward_matrix(), 3), axis=1)
    cosine, sine = rotation_tables()
    vmem = pl.BlockSpec(memory_space=pltpu.VMEM)
    columns = 2 * classes * ANGLES
    return pl.pallas_call(
        functools.partial(spectra_kernel, cycles),
        out_shape=jax.ShapeDtypeStruct((columns, cycles * 128), BF16),
        in_specs=[pl.BlockSpec(memory_space=pltpu.SMEM)] + [vmem] * 4,
        out_specs=vmem,
        scratch_shapes=[pltpu.VMEM((classes * cycles, 128), F32)] * 2,
        compiler_params=pltpu.CompilerParams(vmem_limit_bytes=VMEM_LIMIT),
        cost_estimate=pl.CostEstimate(
            flops=columns * cycles * 128 * 8, bytes_accessed=columns * cycles * 256, transcendentals=0
        ),
        name="rotated_spectra",
    )(inv_noise, refs, jnp.asarray(trio), jnp.asarray(cosine), jnp.asarray(sine))


def bit_reverse(value, bits):
    return sum(((value >> b) & 1) << (bits - 1 - b) for b in range(bits))


def score_kernel(
    cycles,
    slots,
    counts_ref,
    near_ref,
    far_ref,
    offset_ref,
    tc_ref,
    ts_ref,
    forward_ref,
    bt_hbm,
    hat_ref,
    expo_ref,
    stats_ref,
    starts,
    bt_ref,
    plain_ref,
    swap_ref,
    stack_ref,
    sem,
):
    devices = counts_ref.shape[0]
    bits = devices.bit_length() - 1
    me = lax.axis_index("blk")
    chunk = pl.program_id(0)
    copy = pltpu.make_async_copy(bt_hbm, bt_ref, sem)

    @pl.when(chunk == 0)
    def _():
        copy.start()

    def add_start(d, total):
        starts[d] = total
        return total + counts_ref[d]

    lax.fori_loop(0, devices, add_start, jnp.int32(0))

    width = devices // 2 * slots
    lane = lax.broadcasted_iota(jnp.int32, (1, width), 1)
    place = lane % slots
    chosen = None
    for flip, ref in ((0, near_ref), (1, far_ref)):
        rank = jnp.full((1, width), -1, jnp.int32)
        for k in range(devices // 2):
            owner = me ^ (bit_reverse(k, bits) | flip)
            here = (lane // slots == k) & (place < counts_ref[owner])
            rank = jnp.where(here, starts[owner] + place, rank)
        wanted = lax.broadcasted_iota(jnp.int32, (CHUNK, width), 0) + chunk * CHUNK
        pick = (jnp.broadcast_to(rank, (CHUNK, width)) == wanted).astype(F32).astype(BF16)
        term = dot(pick, ref[...])
        chosen = term if chosen is None else chosen + term

    span = cycles * ANGLES
    offset_x = chosen[:, 2 * span : 2 * span + 1]
    offset_y = chosen[:, 2 * span + 1 : 2 * span + 2]
    index = (offset_x + SHIFT // 2) * SHIFT + (offset_y + SHIFT // 2)
    row = lax.broadcasted_iota(jnp.int32, (CHUNK, 96), 1) % 32
    pick = (row.astype(F32) == jnp.broadcast_to(index, (CHUNK, 96))).astype(F32).astype(BF16)
    first = lax.broadcasted_iota(jnp.int32, (CHUNK, 128), 1) < 64
    for jp in range(cycles // 2):
        lanes = slice(jp * 128, jp * 128 + 128)
        cosine = dot(pick, offset_ref[:, lanes])
        sine = dot(pick, offset_ref[:, span + jp * 128 : span + jp * 128 + 128])
        real_in, imag_in = chosen[:, lanes], chosen[:, span + jp * 128 : span + jp * 128 + 128]
        real = real_in * cosine + imag_in * sine
        imag = imag_in * cosine - real_in * sine
        real_roll, imag_roll = pltpu.roll(real, 64, 1), pltpu.roll(imag, 64, 1)
        plain_ref[jp, :, :128] = jnp.where(first, real, imag_roll)
        plain_ref[jp, :, 128:] = jnp.where(first, real_roll, imag)
        swap_ref[jp, :, :128] = jnp.where(first, imag, real_roll)
        swap_ref[jp, :, 128:] = jnp.where(first, imag_roll, real)

    def transform(jp, carry):
        lanes = pl.ds(pl.multiple_of(jp * PAIR, PAIR), PAIR)
        plain, swapped = plain_ref[jp], swap_ref[jp]
        for t in range(STEPS):
            y = plain * tc_ref[t : t + 1, lanes] + swapped * ts_ref[t : t + 1, lanes]
            high, low = halves(y)
            rows = slice(t * CHUNK, (t + 1) * CHUNK)
            stack_ref[0, rows, :128] = high[:, :128]
            stack_ref[0, rows, 128:] = low[:, :128]
            stack_ref[1, rows, :128] = high[:, 128:]
            stack_ref[1, rows, 128:] = low[:, 128:]
        for parity in range(2):
            both = dot(stack_ref[parity], forward_ref[...])
            columns = pl.ds(pl.multiple_of(jp * PAIR + parity * 128, 128), 128)
            hat_ref[0, :, columns] = (both[:, :128] + both[:, 128:]).astype(BF16)
        return carry

    lax.fori_loop(0, cycles // 2, transform, 0)

    @pl.when(chunk == 0)
    def _():
        copy.wait()

    columns = expo_ref.shape[2]
    group = 5 * CHUNK

    def score(i, top):
        rows = pl.ds(pl.multiple_of(i * group, group), group)
        both = dot(hat_ref[0, rows, :], bt_ref[...], ((1,), (1,)))
        scores = both[:, :columns] + both[:, columns:]
        expo_ref[0, rows, :] = scores
        for t in range(5):
            top = jnp.maximum(top, scores[t * CHUNK : (t + 1) * CHUNK])
        return top

    top = lax.fori_loop(0, STEPS // 5, score, jnp.full((CHUNK, columns), -jnp.inf, F32))
    peak = jnp.max(top, axis=1, keepdims=True)

    def exponent(t, total):
        rows = pl.ds(pl.multiple_of(t * CHUNK, CHUNK), CHUNK)
        value = jnp.exp(expo_ref[0, rows, :] - peak)
        expo_ref[0, rows, :] = value
        return total + value

    total = lax.fori_loop(0, STEPS, exponent, jnp.zeros((CHUNK, columns), F32))
    mass = jnp.sum(total, axis=1, keepdims=True)
    diagonal = lax.broadcasted_iota(jnp.int32, (CHUNK, 128), 0) == lax.broadcasted_iota(
        jnp.int32, (CHUNK, 128), 1
    )
    peak_row = jnp.sum(jnp.where(diagonal, peak, 0.0), axis=0, keepdims=True)
    mass_row = jnp.sum(jnp.where(diagonal, mass, 0.0), axis=0, keepdims=True)
    which = lax.broadcasted_iota(jnp.int32, (8, 128), 0)
    tile = jnp.where(which == 0, peak_row, jnp.where(which == 1, mass_row, 0.0))
    stats_ref[...] = jnp.broadcast_to(tile[None, None], stats_ref.shape)


def local_scores(near, far, counts, spectra, cycles, slots, chunks):
    devices = counts.shape[0]
    columns = spectra.shape[0] // 2
    tc, ts = step_tables(cycles)
    whole = lambda shape: pl.BlockSpec(shape, lambda c: (0,) * len(shape))
    table = offset_table(cycles)
    return pl.pallas_call(
        functools.partial(score_kernel, cycles, slots),
        grid=(chunks,),
        out_shape=(
            jax.ShapeDtypeStruct((chunks, ROWS, cycles * 128), BF16),
            jax.ShapeDtypeStruct((chunks, ROWS, columns), F32),
            jax.ShapeDtypeStruct((devices, chunks, 8, 128), F32),
        ),
        in_specs=[
            pl.BlockSpec(memory_space=pltpu.SMEM),
            whole(near.shape),
            whole(far.shape),
            whole(table.shape),
            whole(tc.shape),
            whole(ts.shape),
            whole((256, 256)),
            pl.BlockSpec(memory_space=pl.ANY),
        ],
        out_specs=(
            pl.BlockSpec((1, ROWS, cycles * 128), lambda c: (c, 0, 0)),
            pl.BlockSpec((1, ROWS, columns), lambda c: (c, 0, 0)),
            pl.BlockSpec((devices, 1, 8, 128), lambda c: (0, c, 0, 0)),
        ),
        scratch_shapes=[
            pltpu.SMEM((devices,), jnp.int32),
            pltpu.VMEM(spectra.shape, BF16),
            pltpu.VMEM((cycles // 2, CHUNK, PAIR), F32),
            pltpu.VMEM((cycles // 2, CHUNK, PAIR), F32),
            pltpu.VMEM((2, ROWS, 256), BF16),
            pltpu.SemaphoreType.DMA,
        ],
        compiler_params=pltpu.CompilerParams(vmem_limit_bytes=VMEM_LIMIT),
        name="local_scores",
    )(
        counts,
        near,
        far,
        jnp.asarray(table),
        jnp.asarray(tc),
        jnp.asarray(ts),
        jnp.asarray(forward_stack()),
        spectra,
    )


def sum_kernel(
    classes, counts_ref, stats_ref, expo_ref, hat_ref, cos_ref, sin_ref, image_ref, loglik_ref, out_ref,
    weight_ref, sums_ref,
):
    chunk, jp = pl.program_id(0), pl.program_id(1)
    pairs = pl.num_programs(1)
    me = lax.axis_index("blk")
    columns = classes * ANGLES

    @pl.when(jp == 0)
    def _():
        peaks = stats_ref[:, chunk, 0, :]
        masses = stats_ref[:, chunk, 1, :]
        own_peak = stats_ref[pl.ds(me, 1), chunk, 0, :]
        peak = jnp.max(peaks, axis=0, keepdims=True)
        loglik = peak + jnp.log(jnp.sum(masses * jnp.exp(peaks - peak), axis=0, keepdims=True))
        diagonal = lax.broadcasted_iota(jnp.int32, (CHUNK, 128), 0) == lax.broadcasted_iota(
            jnp.int32, (CHUNK, 128), 1
        )
        column = lambda r: jnp.sum(jnp.where(diagonal, r, 0.0), axis=1, keepdims=True)
        scale = column(jnp.exp(own_peak - loglik))

        def add_start(d, total):
            return total + jnp.where(d < me, counts_ref[d], 0)

        start = lax.fori_loop(0, counts_ref.shape[0], add_start, jnp.int32(0))
        rank = lax.broadcasted_iota(jnp.int32, (CHUNK, 128), 0) + chunk * CHUNK
        slot = lax.broadcasted_iota(jnp.int32, (CHUNK, 128), 1)
        mine = (rank == slot + start) & (slot < counts_ref[me])
        found = jnp.sum(jnp.where(mine, column(loglik), 0.0), axis=0, keepdims=True)

        @pl.when(chunk == 0)
        def _():
            loglik_ref[...] = jnp.zeros_like(loglik_ref)

        loglik_ref[...] += jnp.broadcast_to(found, loglik_ref.shape)

        repeated = jnp.concatenate([scale] * 8, axis=0)

        def weigh(value, width, at):
            high, low = halves(value.T)
            weight_ref[:columns, at : at + width] = high[:, :width]
            weight_ref[columns:, at : at + width] = low[:, :width]

        for block in range(ROWS // 384):
            value = expo_ref[0, block * 384 : (block + 1) * 384, :] * repeated
            for part in range(3):
                weigh(value[part * 128 : (part + 1) * 128], 128, block * 384 + part * 128)
        rest = ROWS % 384
        if rest:
            at = ROWS - rest
            value = expo_ref[0, at:, :] * repeated[:rest]
            value = jnp.concatenate([value, jnp.zeros((128 - rest, columns), F32)], axis=0)
            weigh(value, rest, at)

    both = dot(weight_ref[...], hat_ref[0])
    total = both[:columns] + both[columns:]
    first = lax.broadcasted_iota(jnp.int32, (1, 128), 1) < 64
    height = sums_ref.shape[1]
    rows = []
    for c in range(classes):
        block = total[c * ANGLES : (c + 1) * ANGLES]
        even = jnp.sum(block * cos_ref[...], axis=0, keepdims=True)
        odd = jnp.sum(block * sin_ref[...], axis=0, keepdims=True)
        parts = []
        for parity in range(2):
            lanes = slice(parity * 128, parity * 128 + 128)
            turned = pltpu.roll(odd[:, lanes], 64, 1)
            parts.append(even[:, lanes] + jnp.where(first, -turned, turned))
        rows.append(jnp.concatenate(parts, axis=1))
    if height > classes:
        rows.append(jnp.zeros((height - classes, PAIR), F32))
    value = jnp.concatenate(rows, axis=0)

    @pl.when(chunk == 0)
    def _():
        sums_ref[jp] = value

    @pl.when(chunk > 0)
    def _():
        sums_ref[jp] += value

    @pl.when((chunk == pl.num_programs(0) - 1) & (jp == pairs - 1))
    def _():
        high, low = halves(sums_ref[...].reshape(-1, PAIR))
        upper = dot(high, image_ref[...])
        image = upper[:, :PAIR] + (upper[:, PAIR:] + dot(low, image_ref[:, :PAIR]))
        for q in range(sums_ref.shape[0]):
            for e in range(2):
                out_ref[:, e, q * 128 : (q + 1) * 128] = image[
                    q * height : q * height + classes, e * 128 : (e + 1) * 128
                ]


def local_sums(counts, stats, expo, hat, classes, cycles):
    devices, chunks = stats.shape[:2]
    columns = classes * ANGLES
    pairs = cycles // 2
    cosine, sine = gather_tables()
    whole = lambda shape: pl.BlockSpec(shape, lambda c, j: (0,) * len(shape))
    return pl.pallas_call(
        functools.partial(sum_kernel, classes),
        grid=(chunks, pairs),
        out_shape=(
            jax.ShapeDtypeStruct((8, 128), F32),
            jax.ShapeDtypeStruct((classes, 2, cycles * ANGLES), F32),
        ),
        in_specs=[
            pl.BlockSpec(memory_space=pltpu.SMEM),
            whole(stats.shape),
            pl.BlockSpec((1, ROWS, columns), lambda c, j: (c, 0, 0)),
            pl.BlockSpec((1, ROWS, PAIR), lambda c, j: (c, 0, j)),
            whole((ANGLES, PAIR)),
            whole((ANGLES, PAIR)),
            whole((PAIR, 2 * PAIR)),
        ],
        out_specs=(whole((8, 128)), whole((classes, 2, cycles * ANGLES))),
        scratch_shapes=[
            pltpu.VMEM((2 * columns, ROWS), BF16),
            pltpu.VMEM((pairs, -(-classes // 8) * 8, PAIR), F32),
        ],
        compiler_params=pltpu.CompilerParams(vmem_limit_bytes=VMEM_LIMIT),
        name="local_sums",
    )(counts, stats, expo, hat, jnp.asarray(cosine), jnp.asarray(sine), jnp.asarray(image_stack()))


def local(particles, offsets, references, inv_noise, counts):
    devices = lax.axis_size("blk")
    slots = particles.shape[0]
    cycles = particles.shape[2] // ANGLES
    chunks = MEAN * devices // CHUNK
    classes = references.shape[0]
    spectra = rotated_spectra(references, inv_noise, cycles)
    packed = jnp.concatenate(
        [
            particles.reshape(slots, 2 * cycles * ANGLES),
            jnp.pad(offsets.T.astype(BF16), ((0, 0), (0, 126))),
        ],
        axis=1,
    )
    distance = devices // 2
    while True:
        moved = lax.ppermute(packed, "blk", [(i, i ^ distance) for i in range(devices)])
        if distance == 1:
            break
        packed = jnp.concatenate([packed, moved], axis=0)
        distance //= 2
    hat, expo, stats = local_scores(packed, moved, counts, spectra, cycles, slots, chunks)
    stats = lax.all_to_all(stats, "blk", 0, 0, tiled=True)
    loglik, class_sums = local_sums(counts, stats, expo, hat, classes, cycles)
    return (loglik[0, :slots], class_sums)


def solution(mesh):
    return jax.shard_map(
        local,
        mesh=mesh,
        in_specs=(
            P(("parts", "blk"), None, None),
            P(None, ("parts", "blk")),
            P(("parts", "blk"), None, None),
            P(),
            P("parts"),
        ),
        out_specs=(P(("parts", "blk")), P(("parts", "blk"), None, None)),
        check_vma=False,
    )
```

profile of v0, /device:TPU:0, one launch (start us, length us, event | category | flops | bytes accessed | tf_op | source)
XLA Modules:
  0.0 85.1 jit_solution(8631908012604423231)
XLA Ops:
  0.6 0.7 convert_element_type.8
  1.3 0.1 copy.19
  1.4 0.0 copy-start.2
  1.4 0.9 %copy.21 = bf16[1,8,2,2048]{3,1,2,0:T(8,128)(2,1)S(1)} copy(bf16[1,8,2,2048]{3,2,1,0:T(2,128)(2,1)} %bitcast.13) | data formatting | bytes 131072
  2.3 4.1 %collective-permute-start = (bf16[8,4224]{1,0:T(8,128)(2,1)S(1)}, bf16[8,4224]{1,0:T(8,128)(2,1)S(1)}, u32[]{:S(2)}, u32[]{:S(2)}) collective-permute-start(bf16[8,4224]{1,0:T(8,128)(2,1)S(1)} %pad_maximum_fusion.3), channel_id=1, source_target_pairs={{0,8},{1,9},{2,10},{3,11},{4,12},{5,13},{6,14},{7,15},{8,0},{9,1},... | collective-permute-start | bytes 202760 | tf_op jit(solution)/shard_map/ppermute | solution.py:484
  6.4 3.7 %collective-permute-done = bf16[8,4224]{1,0:T(8,128)(2,1)S(1)} collective-permute-done((bf16[8,4224]{1,0:T(8,128)(2,1)S(1)}, bf16[8,4224]{1,0:T(8,128)(2,1)S(1)}, u32[]{:S(2)}, u32[]{:S(2)}) %collective-permute-start) | collective-permute-done | bytes 67616 | tf_op jit(solution)/shard_map/ppermute | solution.py:484
  10.1 0.7 collective-permute-start.1
  10.8 4.4 %collective-permute-done.1 = bf16[16,4224]{1,0:T(8,128)(2,1)S(1)} collective-permute-done((bf16[16,4224]{1,0:T(8,128)(2,1)S(1)}, bf16[16,4224]{1,0:T(8,128)(2,1)S(1)}, u32[]{:S(2)}, u32[]{:S(2)}) %collective-permute-start.1) | collective-permute-done | bytes 135200 | tf_op jit(solution)/shard_map/ppermute | solution.py:484
  15.2 1.8 %collective-permute-start.2 = (bf16[32,4224]{1,0:T(8,128)(2,1)S(1)}, bf16[32,4224]{1,0:T(8,128)(2,1)S(1)}, u32[]{:S(2)}, u32[]{:S(2)}) collective-permute-start(bf16[32,4224]{1,0:T(8,128)(2,1)S(1)} %pad_maximum_fusion.1), channel_id=1, source_target_pairs={{0,2},{1,3},{2,0},{3,1},{4,6},{5,7},{6,4},{7,5},{8,10},{9,11},{10,... | collective-permute-start | bytes 811016 | tf_op jit(solution)/shard_map/ppermute | solution.py:484
  17.0 4.7 %collective-permute-done.2 = bf16[32,4224]{1,0:T(8,128)(2,1)S(1)} collective-permute-done((bf16[32,4224]{1,0:T(8,128)(2,1)S(1)}, bf16[32,4224]{1,0:T(8,128)(2,1)S(1)}, u32[]{:S(2)}, u32[]{:S(2)}) %collective-permute-start.2) | collective-permute-done | bytes 270368 | tf_op jit(solution)/shard_map/ppermute | solution.py:484
  21.8 0.0 copy-start
  21.8 0.1 collective-permute-start.3
  21.9 0.0 copy-done.2
  21.9 0.1 reshape.14
  22.0 0.1 copy.23
  22.1 0.7 reshape.15.refs_ref
  22.8 4.8 %rotated_spectra.1.bt_hbm = bf16[512,4096]{1,0:T(8,128)(2,1)} custom-call(f32[32]{0:T(128)} %noise_ref.1, bf16[128,128]{1,0:T(8,128)(2,1)} %reshape.15.refs_ref, bf16[128,384]{1,0:T(8,128)(2,1)} %constant.23.clone.trio_ref, f32[64,128]{1,0:T(8,128)} %constant.24.clone.cos_ref, f32[64,128]{1,0:T(8,128)} %constant.25.clone.sin_ref), custom_call_target="tpu_custom_call" | custom-call | flops 16777216 | bytes 4194304 | tf_op jit(solution)/shard_map/rotated_spectra/pallas_call | solution.py:145
  27.6 0.0 copy-done
  27.6 0.0 collective-permute-done.3.far_ref
  27.6 0.0 copy-start.1
  27.6 0.8 copy-done.1
  28.4 25.3 %local_scores.1 = (bf16[1,1200,4096]{2,1,0:T(8,128)(2,1)}, f32[1,1200,256]{2,1,0:T(8,128)}, f32[16,1,8,128]{3,2,1,0:T(8,128)}) custom-call(s32[16]{0:T(128)} %counts_ref.3, bf16[64,4224]{1,0:T(8,128)(2,1)} %copy-done, bf16[64,4224]{1,0:T(8,128)(2,1)} %copy-done.1, bf16[96,4096]{1,0:T(8,128)(2,1)} %constant.26.clone.offset_ref, ...), custom_call_target="tpu_custom_call" | custom-call | tf_op jit(solution)/shard_map/local_scores/pallas_call | solution.py:297
  53.7 13.7 %all_to_all.5.stats_ref = f32[16,1,8,128]{3,2,1,0:T(8,128)} all-to-all(f32[16,1,8,128]{3,2,1,0:T(8,128)} %get-tuple-element.7), channel_id=1, replica_groups=mesh['parts'=2,'blk'=16] {'blk'}, dimensions={0} | all-to-all | bytes 131072 | tf_op jit(solution)/shard_map/all_to_all | solution.py:490
  67.5 16.4 %local_sums.1 = (f32[8,128]{1,0:T(8,128)}, f32[4,2,2048]{2,1,0:T(2,128)}) custom-call(s32[16]{0:T(128)} %counts_ref.3, f32[16,1,8,128]{3,2,1,0:T(8,128)} %all_to_all.5.stats_ref, f32[1,1200,256]{2,1,0:T(8,128)} %get-tuple-element.8.expo_ref, bf16[1,1200,4096]{2,1,0:T(8,128)(2,1)} %get-tuple-element.9.hat_ref, f32[64,256]{1,0:T(8,128)} %constant.30.clone.cos_ref, ...), custom_call_target="tpu_custom_call" | custom-call | tf_op jit(solution)/shard_map/local_sums/pallas_call | solution.py:442
  83.9 1.2 %slice_bitcast_fusion = f32[8]{0:T(128)} fusion(f32[8,128]{1,0:T(8,128)} %get-tuple-element.10), kind=kLoop, calls=%fused_computation.5 | loop fusion | bytes 64 | tf_op jit(solution)/shard_map/squeeze | solution.py:492
  (5 shorter events, 0.1 us)
Async XLA Ops:
  1.4 20.5 %copy-start.2 = (bf16[4,2,2048]{2,1,0:T(2,128)(2,1)S(1)}, bf16[4,2,2048]{2,1,0:T(2,128)(2,1)}, u32[]{:S(2)}) copy-start(bf16[4,2,2048]{2,1,0:T(2,128)(2,1)} %param.17) | copy-start | bytes 98308
  2.3 7.8 %collective-permute-start = (bf16[8,4224]{1,0:T(8,128)(2,1)S(1)}, bf16[8,4224]{1,0:T(8,128)(2,1)S(1)}, u32[]{:S(2)}, u32[]{:S(2)}) collective-permute-start(bf16[8,4224]{1,0:T(8,128)(2,1)S(1)} %pad_maximum_fusion.3), channel_id=1, source_target_pairs={{0,8},{1,9},{2,10},{3,11},{4,12},{5,13},{6,14},{7,15},{8,0},{9,1},... | collective-permute-start | bytes 202760 | tf_op jit(solution)/shard_map/ppermute | solution.py:484
  10.1 5.1 %collective-permute-start.1 = (bf16[16,4224]{1,0:T(8,128)(2,1)S(1)}, bf16[16,4224]{1,0:T(8,128)(2,1)S(1)}, u32[]{:S(2)}, u32[]{:S(2)}) collective-permute-start(bf16[16,4224]{1,0:T(8,128)(2,1)S(1)} %pad_maximum_fusion.2), channel_id=1, source_target_pairs={{0,4},{1,5},{2,6},{3,7},{4,0},{5,1},{6,2},{7,3},{8,12},{9,13},{10,... | collective-permute-start | bytes 405512 | tf_op jit(solution)/shard_map/ppermute | solution.py:484
  15.2 6.5 %collective-permute-start.2 = (bf16[32,4224]{1,0:T(8,128)(2,1)S(1)}, bf16[32,4224]{1,0:T(8,128)(2,1)S(1)}, u32[]{:S(2)}, u32[]{:S(2)}) collective-permute-start(bf16[32,4224]{1,0:T(8,128)(2,1)S(1)} %pad_maximum_fusion.1), channel_id=1, source_target_pairs={{0,2},{1,3},{2,0},{3,1},{4,6},{5,7},{6,4},{7,5},{8,10},{9,11},{10,... | collective-permute-start | bytes 811016 | tf_op jit(solution)/shard_map/ppermute | solution.py:484
  21.8 5.8 %copy-start = (bf16[64,4224]{1,0:T(8,128)(2,1)}, bf16[64,4224]{1,0:T(8,128)(2,1)S(1)}, u32[]{:S(2)}) copy-start(bf16[64,4224]{1,0:T(8,128)(2,1)S(1)} %pad_maximum_fusion.near_ref) | copy-start | bytes 1622020
  21.8 5.8 %collective-permute-start.3 = (bf16[64,4224]{1,0:T(8,128)(2,1)S(1)}, bf16[64,4224]{1,0:T(8,128)(2,1)S(1)}, u32[]{:S(2)}, u32[]{:S(2)}) collective-permute-start(bf16[64,4224]{1,0:T(8,128)(2,1)S(1)} %pad_maximum_fusion.near_ref), channel_id=1, source_target_pairs={{0,1},{1,0},{2,3},{3,2},{4,5},{5,4},{6,7},{7,6},{8,9},{9,8},{10,11... | collective-permute-start | bytes 1622024 | tf_op jit(solution)/shard_map/ppermute | solution.py:484
  27.6 0.8 copy-start.1
where the time goes:
time: 85.7 us; the launch traced here: 85.1 us
  Pallas kernels  46.5 us (54%)
  blocking collectives  13.7 us (16%)
  waiting for transfers between devices  12.9 us (15%)
  starting transfers between devices  6.62 us (8%)
  local copies, waits for them, and re-layouts  3.89 us (5%)
    pallas_call x1, Pallas kernels, local_scores(): pl.pallas_call(functools.partial(score_kernel, cycles, slots), grid=(chun...  25.3 us
    pallas_call x1, Pallas kernels, local_sums(): pl.pallas_call(functools.partial(sum_kernel, classes), grid=(chunks, pair...  16.4 us
    all_to_all x1, blocking collectives, local(): stats = lax.all_to_all(stats, 'blk', 0, 0, tiled=True)  13.7 us
    ppermute x4, waiting for transfers between devices, local(): lax.ppermute(packed, 'blk', [(i, i ^ distance) for i in range(devices)])  12.9 us
    ppermute x4, starting transfers between devices, local(): lax.ppermute(packed, 'blk', [(i, i ^ distance) for i in range(devices)])  6.62 us
    pallas_call x1, Pallas kernels, rotated_spectra(): pl.pallas_call(functools.partial(spectra_kernel, cycles), out_shape=jax.S...  4.77 us
    unnamed x7, local copies, waits for them, and re-layouts  1.71 us
  transfers between devices with their start and end apart: 4, of which 3 were waited for; matrix products, arithmetic and copies ran while one was open for 1% of the time, Pallas kernels for 6%

commit v1 on v0

v1 whole, which is shorter than its diff:
```python
import functools
import math

import jax
import jax.numpy as jnp
import numpy as np
from jax import lax
from jax.experimental import pallas as pl
from jax.experimental.pallas import tpu as pltpu
from jax.sharding import PartitionSpec as P

ANGLES = 64
SHIFT = 5
STEPS = SHIFT * SHIFT
MEAN = 3
CHUNK = 48
ROWS = STEPS * CHUNK
PAIR = 4 * ANGLES
WIDE = 16
STEP_GROUPS = tuple(tuple(g) for g in (range(i, min(i + 9, STEPS)) for i in range(0, STEPS, 9)))
F32 = jnp.float32
BF16 = jnp.bfloat16
MIB = 1024 * 1024


def split(table, terms):
    rest = np.asarray(table, np.float64)
    out = []
    for _ in range(terms):
        piece = rest.astype(np.float32).astype(jnp.bfloat16)
        out.append(piece)
        rest = rest - piece.astype(np.float64)
    return out


def angle_products():
    index = np.arange(ANGLES)
    radians = 2.0 * math.pi / ANGLES * (index[:, None] * index[None, :] % ANGLES)
    return np.cos(radians), np.sin(radians)


def step_phases(cycles):
    polar = 2.0 * math.pi / ANGLES * np.arange(ANGLES)
    radius = np.arange(1, cycles + 1)
    step = np.arange(STEPS)
    along = (step // SHIFT - SHIFT // 2)[:, None] * np.cos(polar) + (step % SHIFT - SHIFT // 2)[
        :, None
    ] * np.sin(polar)
    phases = 2.0 * math.pi / 128.0 * radius[None, :, None] * along[:, None, :]
    return np.cos(phases), np.sin(phases)


def step_tables(cycles):
    cosine, sine = step_phases(cycles)
    tc = np.concatenate([cosine, cosine], axis=2).reshape(STEPS, -1).astype(np.float32)
    ts = np.concatenate([sine, -sine], axis=2).reshape(STEPS, -1).astype(np.float32)
    return tc, ts


def offset_table(cycles):
    cosine, sine = step_phases(cycles)
    both = np.concatenate([cosine.reshape(STEPS, -1), sine.reshape(STEPS, -1)], axis=1)
    both = np.pad(both, ((0, 32 - STEPS), (0, 0)))
    return np.concatenate(split(both, 3), axis=0)


def forward_matrix():
    cosine, sine = angle_products()
    return np.block([[cosine, -sine], [sine, cosine]])


def forward_stack():
    high, low = split(forward_matrix(), 2)
    return np.block([[high, low], [high, np.zeros_like(low)]])


def rotation_tables():
    cosine, sine = angle_products()
    cosine, sine = cosine / ANGLES, sine / ANGLES
    return (
        np.concatenate([cosine, cosine], axis=1).astype(np.float32),
        np.concatenate([sine, -sine], axis=1).astype(np.float32),
    )


def gather_tables():
    cosine, sine = angle_products()
    return (
        np.concatenate([cosine] * 4, axis=1).astype(np.float32),
        np.concatenate([sine] * 4, axis=1).astype(np.float32),
    )


def image_stack():
    cosine, sine = angle_products()
    table = np.zeros((2, 2, ANGLES, 2, 2, ANGLES))
    for parity in range(2):
        table[parity, 0, :, 0, parity] = cosine / ANGLES
        table[parity, 1, :, 0, parity] = -sine / ANGLES
        table[parity, 0, :, 1, parity] = sine / ANGLES
        table[parity, 1, :, 1, parity] = cosine / ANGLES
    high, low = split(table.reshape(PAIR, PAIR), 2)
    return np.concatenate([high, low], axis=1)


def dot(left, right, dims=((1,), (0,))):
    return lax.dot_general(left, right, (dims, ((), ())), preferred_element_type=F32)


def halves(value):
    high = value.astype(BF16)
    return high, (value - high.astype(F32)).astype(BF16)


def spectra_kernel(cycles, noise_ref, refs_ref, trio_ref, cos_ref, sin_ref, bt_ref, hat_ref, swap_ref):
    classes = refs_ref.shape[0] // cycles
    raw = dot(refs_ref[...], trio_ref[...])
    hat = (raw[:, :128] + raw[:, 128:256]) + raw[:, 256:]
    hat_ref[...] = hat
    swap_ref[...] = pltpu.roll(hat, 64, 1)
    cosine, sine = cos_ref[...], sin_ref[...]
    columns = classes * ANGLES

    def body(j, carry):
        weight = noise_ref[j]
        lanes = pl.ds(pl.multiple_of(j * 128, 128), 128)
        for c in range(classes):
            row = pl.ds(c * cycles + j, 1)
            plain = (hat_ref[row, :] * weight).astype(BF16).astype(F32)
            swapped = (swap_ref[row, :] * weight).astype(BF16).astype(F32)
            high, low = halves(plain * cosine + swapped * sine)
            bt_ref[c * ANGLES : (c + 1) * ANGLES, lanes] = high
            bt_ref[columns + c * ANGLES : columns + (c + 1) * ANGLES, lanes] = low
        return carry

    lax.fori_loop(0, cycles, body, 0)


def rotated_spectra(references, inv_noise, cycles):
    classes = references.shape[0]
    refs = references.reshape(classes, 2, cycles, ANGLES).transpose(0, 2, 1, 3)
    refs = refs.reshape(classes * cycles, 2 * ANGLES)
    trio = np.concatenate(split(forward_matrix(), 3), axis=1)
    cosine, sine = rotation_tables()
    vmem = pl.BlockSpec(memory_space=pltpu.VMEM)
    columns = 2 * classes * ANGLES
    return pl.pallas_call(
        functools.partial(spectra_kernel, cycles),
        out_shape=pltpu.VMEM((columns, cycles * 128), BF16),
        in_specs=[pl.BlockSpec(memory_space=pltpu.SMEM)] + [vmem] * 4,
        out_specs=vmem,
        scratch_shapes=[pltpu.VMEM((classes * cycles, 128), F32)] * 2,
        compiler_params=pltpu.CompilerParams(vmem_limit_bytes=16 * MIB),
        cost_estimate=pl.CostEstimate(
            flops=columns * cycles * 128 * 8, bytes_accessed=columns * cycles * 256, transcendentals=0
        ),
        name="rotated_spectra",
    )(inv_noise, refs, jnp.asarray(trio), jnp.asarray(cosine), jnp.asarray(sine))


def bit_reverse(value, bits):
    return sum(((value >> b) & 1) << (bits - 1 - b) for b in range(bits))


def pack_kernel(particles_hbm, offsets_hbm, out_ref, particles_ref, offsets_ref, sems):
    slots, span = particles_ref.shape[0], particles_ref.shape[2]
    copies = [
        pltpu.make_async_copy(particles_hbm, particles_ref, sems.at[0]),
        pltpu.make_async_copy(offsets_hbm, offsets_ref, sems.at[1]),
    ]
    for copy in copies:
        copy.start()
    for copy in copies:
        copy.wait()
    values = particles_ref[...].astype(F32)
    out_ref[:, :span] = values[:, 0, :].astype(BF16)
    out_ref[:, span : 2 * span] = values[:, 1, :].astype(BF16)
    offsets = offsets_ref[...].astype(F32)
    diagonal = lax.broadcasted_iota(jnp.int32, (slots, slots), 0) == lax.broadcasted_iota(
        jnp.int32, (slots, slots), 1
    )
    lane = lax.broadcasted_iota(jnp.int32, (slots, 128), 1)
    tail = jnp.zeros((slots, 128), F32)
    for axis in range(2):
        column = jnp.sum(jnp.where(diagonal, offsets[axis : axis + 1], 0.0), axis=1, keepdims=True)
        tail = jnp.where(lane == axis, column, tail)
    out_ref[:, 2 * span :] = tail.astype(BF16)


def pack(particles, offsets):
    slots, _, span = particles.shape
    vmem = pl.BlockSpec(memory_space=pltpu.VMEM)
    return pl.pallas_call(
        pack_kernel,
        out_shape=pltpu.VMEM((slots, 2 * span + 128), BF16),
        in_specs=[pl.BlockSpec(memory_space=pltpu.HBM)] * 2,
        out_specs=vmem,
        scratch_shapes=[
            pltpu.VMEM(particles.shape, particles.dtype),
            pltpu.VMEM(offsets.shape, offsets.dtype),
            pltpu.SemaphoreType.DMA((2,)),
        ],
        compiler_params=pltpu.CompilerParams(vmem_limit_bytes=2 * 1024 * 1024),
        name="pack",
    )(
        pltpu.with_memory_space_constraint(particles, pltpu.HBM),
        pltpu.with_memory_space_constraint(offsets, pltpu.HBM),
    )


def find_starts(counts_ref, starts):
    def add_start(d, total):
        starts[d] = total
        return total + counts_ref[d]

    lax.fori_loop(0, counts_ref.shape[0], add_start, jnp.int32(0))


def score_chunk(
    cycles, slots, chunk, counts_ref, near_ref, far_ref, offset_ref, tc_ref, ts_ref, forward_ref, bt_ref,
    hat_ref, expo_ref, stats_ref, starts, plain_ref, swap_ref, stack_ref,
):
    devices = counts_ref.shape[0]
    bits = devices.bit_length() - 1
    me = lax.axis_index("blk")
    width = devices // 2 * slots
    lane = lax.broadcasted_iota(jnp.int32, (1, width), 1)
    place = lane % slots
    chosen = None
    for flip, ref in ((0, near_ref), (1, far_ref)):
        rank = jnp.full((1, width), -1, jnp.int32)
        for k in range(devices // 2):
            owner = me ^ (bit_reverse(k, bits) | flip)
            here = (lane // slots == k) & (place < counts_ref[owner])
            rank = jnp.where(here, starts[owner] + place, rank)
        wanted = lax.broadcasted_iota(jnp.int32, (CHUNK, width), 0) + chunk * CHUNK
        pick = (jnp.broadcast_to(rank, (CHUNK, width)) == wanted).astype(F32).astype(BF16)
        term = dot(pick, ref[...])
        chosen = term if chosen is None else chosen + term

    span = cycles * ANGLES
    offset_x = chosen[:, 2 * span : 2 * span + 1]
    offset_y = chosen[:, 2 * span + 1 : 2 * span + 2]
    index = (offset_x + SHIFT // 2) * SHIFT + (offset_y + SHIFT // 2)
    row = lax.broadcasted_iota(jnp.int32, (CHUNK, 96), 1) % 32
    pick = (row.astype(F32) == jnp.broadcast_to(index, (CHUNK, 96))).astype(F32).astype(BF16)
    first = lax.broadcasted_iota(jnp.int32, (CHUNK, 128), 1) < 64
    for jp in range(cycles // 2):
        lanes = slice(jp * 128, jp * 128 + 128)
        cosine = dot(pick, offset_ref[:, lanes])
        sine = dot(pick, offset_ref[:, span + jp * 128 : span + jp * 128 + 128])
        real_in, imag_in = chosen[:, lanes], chosen[:, span + jp * 128 : span + jp * 128 + 128]
        real = real_in * cosine + imag_in * sine
        imag = imag_in * cosine - real_in * sine
        real_roll, imag_roll = pltpu.roll(real, 64, 1), pltpu.roll(imag, 64, 1)
        plain_ref[jp, :, :128] = jnp.where(first, real, imag_roll)
        plain_ref[jp, :, 128:] = jnp.where(first, real_roll, imag)
        swap_ref[jp, :, :128] = jnp.where(first, imag, real_roll)
        swap_ref[jp, :, 128:] = jnp.where(first, imag_roll, real)

    def transform(jp, carry):
        lanes = pl.ds(pl.multiple_of(jp * PAIR, PAIR), PAIR)
        plain, swapped = plain_ref[jp], swap_ref[jp]
        for steps in STEP_GROUPS:
            for t in steps:
                y = plain * tc_ref[t : t + 1, lanes] + swapped * ts_ref[t : t + 1, lanes]
                high, low = halves(y)
                rows = slice(t * CHUNK, (t + 1) * CHUNK)
                stack_ref[0, rows, :128] = high[:, :128]
                stack_ref[0, rows, 128:] = low[:, :128]
                stack_ref[1, rows, :128] = high[:, 128:]
                stack_ref[1, rows, 128:] = low[:, 128:]
            rows = slice(steps[0] * CHUNK, (steps[-1] + 1) * CHUNK)
            for parity in range(2):
                both = dot(stack_ref[parity, rows], forward_ref[...])
                columns = pl.ds(pl.multiple_of(jp * PAIR + parity * 128, 128), 128)
                hat_ref[rows, columns] = (both[:, :128] + both[:, 128:]).astype(BF16)
        return carry

    lax.fori_loop(0, cycles // 2, transform, 0)

    columns = expo_ref.shape[1]
    both = dot(hat_ref[...], bt_ref[...], ((1,), (1,)))
    expo_ref[...] = both[:, :columns] + both[:, columns:]
    step_rows = [slice(t * CHUNK, (t + 1) * CHUNK) for t in range(STEPS)]
    top = expo_ref[step_rows[0], :]
    for rows in step_rows[1:]:
        top = jnp.maximum(top, expo_ref[rows, :])
    peak = jnp.max(top, axis=1, keepdims=True)
    total = jnp.zeros((CHUNK, columns), F32)
    for rows in step_rows:
        value = jnp.exp(expo_ref[rows, :] - peak)
        expo_ref[rows, :] = value
        total = total + value
    mass = jnp.sum(total, axis=1, keepdims=True)
    diagonal = lax.broadcasted_iota(jnp.int32, (CHUNK, 128), 0) == lax.broadcasted_iota(
        jnp.int32, (CHUNK, 128), 1
    )
    peak_row = jnp.sum(jnp.where(diagonal, peak, 0.0), axis=0, keepdims=True)
    mass_row = jnp.sum(jnp.where(diagonal, mass, 0.0), axis=0, keepdims=True)
    which = lax.broadcasted_iota(jnp.int32, (8, 128), 0)
    tile = jnp.where(which == 0, peak_row, jnp.where(which == 1, mass_row, 0.0))
    for d in range(devices):
        stats_ref[d, chunk] = tile


def score_kernel(
    cycles, slots, chunks, counts_ref, near_ref, far_ref, offset_ref, tc_ref, ts_ref, forward_ref, bt_ref,
    hat_ref, expo_ref, stats_ref, starts, plain_ref, swap_ref, stack_ref, *spare,
):
    find_starts(counts_ref, starts)
    given = (counts_ref, near_ref, far_ref, offset_ref, tc_ref, ts_ref, forward_ref, bt_ref)
    held = (stats_ref, starts, plain_ref, swap_ref, stack_ref)
    if chunks == 1:
        score_chunk(cycles, slots, 0, *given, hat_ref, expo_ref, *held)
        return
    hat_now, expo_now = spare

    def body(chunk, carry):
        score_chunk(cycles, slots, chunk, *given, hat_now, expo_now, *held)
        pltpu.sync_copy(hat_now, hat_ref.at[chunk])
        pltpu.sync_copy(expo_now, expo_ref.at[chunk])
        return carry

    lax.fori_loop(0, chunks, body, 0)


def local_scores(near, far, counts, spectra, cycles, slots, chunks):
    devices = counts.shape[0]
    columns = spectra.shape[0] // 2
    tc, ts = step_tables(cycles)
    table = offset_table(cycles)
    vmem = pl.BlockSpec(memory_space=pltpu.VMEM)
    hat, expo = (ROWS, cycles * 128), (ROWS, columns)
    if chunks == 1:
        kept = (pltpu.VMEM(hat, BF16), pltpu.VMEM(expo, F32))
        place, spare = vmem, []
    else:
        kept = (
            jax.ShapeDtypeStruct((chunks, *hat), BF16),
            jax.ShapeDtypeStruct((chunks, *expo), F32),
        )
        place, spare = pl.BlockSpec(memory_space=pl.ANY), [pltpu.VMEM(hat, BF16), pltpu.VMEM(expo, F32)]
    return pl.pallas_call(
        functools.partial(score_kernel, cycles, slots, chunks),
        out_shape=(*kept, jax.ShapeDtypeStruct((devices, chunks, 8, 128), F32)),
        in_specs=[pl.BlockSpec(memory_space=pltpu.SMEM)] + [vmem] * 7,
        out_specs=(place, place, vmem),
        scratch_shapes=[
            pltpu.SMEM((devices,), jnp.int32),
            pltpu.VMEM((cycles // 2, CHUNK, PAIR), F32),
            pltpu.VMEM((cycles // 2, CHUNK, PAIR), F32),
            pltpu.VMEM((2, ROWS, 256), BF16),
            *spare,
        ],
        compiler_params=pltpu.CompilerParams(vmem_limit_bytes=(16 if chunks == 1 else 40) * MIB),
        name="local_scores",
    )(
        counts, near, far, jnp.asarray(table), jnp.asarray(tc), jnp.asarray(ts), jnp.asarray(forward_stack()),
        pltpu.with_memory_space_constraint(spectra, pltpu.VMEM),
    )


def sum_chunk(
    classes, chunk, counts_ref, stats_ref, expo_ref, hat_ref, cos_ref, sin_ref, loglik_ref, weight_ref, sums_ref,
):
    slots = loglik_ref.shape[1]
    me = lax.axis_index("blk")
    columns = classes * ANGLES
    peaks = stats_ref[:, chunk, 0, :]
    masses = stats_ref[:, chunk, 1, :]
    own_peak = stats_ref[pl.ds(me, 1), chunk, 0, :]
    peak = jnp.max(peaks, axis=0, keepdims=True)
    loglik = peak + jnp.log(jnp.sum(masses * jnp.exp(peaks - peak), axis=0, keepdims=True))
    diagonal = lax.broadcasted_iota(jnp.int32, (CHUNK, 128), 0) == lax.broadcasted_iota(
        jnp.int32, (CHUNK, 128), 1
    )
    column = lambda r: jnp.sum(jnp.where(diagonal, r, 0.0), axis=1, keepdims=True)
    scale = column(jnp.exp(own_peak - loglik))

    def add_start(d, total):
        return total + jnp.where(d < me, counts_ref[d], 0)

    start = lax.fori_loop(0, counts_ref.shape[0], add_start, jnp.int32(0))
    rank = lax.broadcasted_iota(jnp.int32, (CHUNK, slots), 0) + chunk * CHUNK
    slot = lax.broadcasted_iota(jnp.int32, (CHUNK, slots), 1)
    mine = (rank == slot + start) & (slot < counts_ref[me])
    loglik_ref[...] += jnp.sum(jnp.where(mine, column(loglik), 0.0), axis=0, keepdims=True)

    repeated = jnp.concatenate([scale] * 8, axis=0)

    def weigh(value, width, at):
        high, low = halves(value.T)
        weight_ref[:columns, at : at + width] = high[:, :width]
        weight_ref[columns:, at : at + width] = low[:, :width]

    for block in range(ROWS // 384):
        value = expo_ref[block * 384 : (block + 1) * 384, :] * repeated
        for part in range(3):
            weigh(value[part * 128 : (part + 1) * 128], 128, block * 384 + part * 128)
    rest = ROWS % 384
    if rest:
        at = ROWS - rest
        value = expo_ref[at:, :] * repeated[:rest]
        value = jnp.concatenate([value, jnp.zeros((128 - rest, columns), F32)], axis=0)
        weigh(value, rest, at)

    first = lax.broadcasted_iota(jnp.int32, (1, 128), 1) < 64
    height = sums_ref.shape[1]

    def body(i, carry):
        lanes = pl.ds(pl.multiple_of(i * (WIDE * PAIR), WIDE * PAIR), WIDE * PAIR)
        both = dot(weight_ref[...], hat_ref[:, lanes])
        totals = both[:columns] + both[columns:]
        for q in range(WIDE):
            turn_back(i * WIDE + q, totals[:, q * PAIR : (q + 1) * PAIR])
        return carry

    def turn_back(jp, total):
        rows = []
        for c in range(classes):
            block = total[c * ANGLES : (c + 1) * ANGLES]
            even = jnp.sum(block * cos_ref[...], axis=0, keepdims=True)
            odd = jnp.sum(block * sin_ref[...], axis=0, keepdims=True)
            parts = []
            for parity in range(2):
                part = slice(parity * 128, parity * 128 + 128)
                turned = pltpu.roll(odd[:, part], 64, 1)
                parts.append(even[:, part] + jnp.where(first, -turned, turned))
            rows.append(jnp.concatenate(parts, axis=1))
        if height > classes:
            rows.append(jnp.zeros((height - classes, PAIR), F32))
        sums_ref[jp] += jnp.concatenate(rows, axis=0)

    lax.fori_loop(0, sums_ref.shape[0] // WIDE, body, 0)


def sum_kernel(
    classes, chunks, counts_ref, stats_ref, expo_ref, hat_ref, cos_ref, sin_ref, image_ref, loglik_ref, out_ref,
    weight_ref, sums_ref, *spare,
):
    loglik_ref[...] = jnp.zeros_like(loglik_ref)
    sums_ref[...] = jnp.zeros_like(sums_ref)
    tables = (cos_ref, sin_ref, loglik_ref, weight_ref, sums_ref)
    if chunks == 1:
        sum_chunk(classes, 0, counts_ref, stats_ref, expo_ref, hat_ref, *tables)
    else:
        hat_now, expo_now = spare

        def body(chunk, carry):
            pltpu.sync_copy(hat_ref.at[chunk], hat_now)
            pltpu.sync_copy(expo_ref.at[chunk], expo_now)
            sum_chunk(classes, chunk, counts_ref, stats_ref, expo_now, hat_now, *tables)
            return carry

        lax.fori_loop(0, chunks, body, 0)

    height = sums_ref.shape[1]
    high, low = halves(sums_ref[...].reshape(-1, PAIR))
    upper = dot(high, image_ref[...])
    image = upper[:, :PAIR] + (upper[:, PAIR:] + dot(low, image_ref[:, :PAIR]))
    for q in range(sums_ref.shape[0]):
        for e in range(2):
            out_ref[:, e, q * 128 : (q + 1) * 128] = image[
                q * height : q * height + classes, e * 128 : (e + 1) * 128
            ]


def local_sums(counts, stats, expo, hat, classes, cycles, slots, chunks):
    columns = classes * ANGLES
    pairs = cycles // 2
    cosine, sine = gather_tables()
    vmem = pl.BlockSpec(memory_space=pltpu.VMEM)
    place, spare = vmem, []
    if chunks > 1:
        place = pl.BlockSpec(memory_space=pl.ANY)
        spare = [pltpu.VMEM((ROWS, cycles * 128), BF16), pltpu.VMEM((ROWS, columns), F32)]
    return pl.pallas_call(
        functools.partial(sum_kernel, classes, chunks),
        out_shape=(
            jax.ShapeDtypeStruct((1, slots), F32),
            jax.ShapeDtypeStruct((classes, 2, cycles * ANGLES), F32),
        ),
        in_specs=[pl.BlockSpec(memory_space=pltpu.SMEM), vmem, place, place, vmem, vmem, vmem],
        out_specs=(vmem, vmem),
        scratch_shapes=[
            pltpu.VMEM((2 * columns, ROWS), BF16),
            pltpu.VMEM((pairs, -(-classes // 8) * 8, PAIR), F32),
            *spare,
        ],
        compiler_params=pltpu.CompilerParams(vmem_limit_bytes=(16 if chunks == 1 else 40) * MIB),
        name="local_sums",
    )(counts, stats, expo, hat, jnp.asarray(cosine), jnp.asarray(sine), jnp.asarray(image_stack()))


def local(particles, offsets, references, inv_noise, counts):
    devices = lax.axis_size("blk")
    slots = particles.shape[0]
    cycles = particles.shape[2] // ANGLES
    chunks = MEAN * devices // CHUNK
    classes = references.shape[0]
    packed = pack(particles, offsets)
    distance = devices // 2
    while True:
        if distance == 2:
            moved = lax.ppermute(packed, "blk", [(i, i ^ distance) for i in range(devices)])
            spectra = rotated_spectra(references, inv_noise, cycles)
            moved, spectra = lax.optimization_barrier((moved, spectra))
        else:
            moved = lax.ppermute(packed, "blk", [(i, i ^ distance) for i in range(devices)])
        if distance == 1:
            break
        packed = jnp.concatenate([packed, moved], axis=0)
        distance //= 2
    hat, expo, stats = local_scores(packed, moved, counts, spectra, cycles, slots, chunks)
    stats = lax.all_to_all(stats, "blk", 0, 0, tiled=True)
    loglik, class_sums = local_sums(counts, stats, expo, hat, classes, cycles, slots, chunks)
    return (loglik.reshape(slots), class_sums)


def solution(mesh):
    return jax.shard_map(
        local,
        mesh=mesh,
        in_specs=(
            P(("parts", "blk"), None, None),
            P(None, ("parts", "blk")),
            P(("parts", "blk"), None, None),
            P(),
            P("parts"),
        ),
        out_specs=(P(("parts", "blk")), P(("parts", "blk"), None, None)),
        check_vma=False,
    )
```

time: 85.7 us -> 62.9 us (0.73)
  Pallas kernels: 46.5 us -> 29.3 us
  local copies, waits for them, and re-layouts: 3.89 us -> 1.1 us
  waiting for transfers between devices: 12.9 us -> 11.3 us
    pallas_call x3 -> x4, Pallas kernels: 46.5 us -> 29.3 us  [the longest x1 18.4 us: local_scores(): pl.pallas_call(functools.partial(score_kernel, cycles, slots, chunks), ou...]
    unnamed x7 -> x24, local copies, waits for them, and re-layouts: 1.71 us -> 0.08 us
    ppermute x4, waiting for transfers between devices: 12.9 us -> 11.3 us  [local(): lax.ppermute(packed, 'blk', [(i, i ^ distance) for i in range(devices)])]
    squeeze x1 -> x0, local copies, waits for them, and re-layouts: 1.19 us -> none  [local(): return (loglik[0, :slots], class_sums)]
  transfers between devices with their start and end apart: 4 -> 4, of which waited for: 3 -> 4; matrix products, arithmetic and copies ran while one was open for 1% -> 2% of each run, Pallas kernels for 6% -> 4%
where the time goes in v1:
time: 62.9 us; the launch traced here: 62.6 us
  Pallas kernels  29.3 us (47%)
  blocking collectives  13.3 us (21%)
  waiting for transfers between devices  11.3 us (18%)
  starting transfers between devices  6.62 us (11%)
  local copies, waits for them, and re-layouts  1.1 us (2%)
  between operations  0.83 us (1%)
    pallas_call x1, Pallas kernels, local_scores(): pl.pallas_call(functools.partial(score_kernel, cycles, slots, chunks), ou...  18.4 us
    all_to_all x1, blocking collectives, local(): stats = lax.all_to_all(stats, 'blk', 0, 0, tiled=True)  13.3 us
    ppermute x4, waiting for transfers between devices, local(): lax.ppermute(packed, 'blk', [(i, i ^ distance) for i in range(devices)])  11.3 us
    pallas_call x1, Pallas kernels, local_sums(): pl.pallas_call(functools.partial(sum_kernel, classes, chunks), out_shape=...  7.51 us
    ppermute x4, starting transfers between devices, local(): lax.ppermute(packed, 'blk', [(i, i ^ distance) for i in range(devices)])  6.62 us
    pallas_call x1, Pallas kernels, rotated_spectra(): pl.pallas_call(functools.partial(spectra_kernel, cycles), out_shape=pltpu...  2.31 us
  transfers between devices with their start and end apart: 4, of which 4 were waited for; matrix products, arithmetic and copies ran while one was open for 2% of the time, Pallas kernels for 4%

profile of v1, /device:TPU:0, one launch (start us, length us, event | category | flops | bytes accessed | tf_op | source)
XLA Modules:
  0.0 62.6 jit_solution(1105105481303737483)
XLA Ops:
  0.6 0.0 copy-start.8
  0.6 0.0 copy-start.9
  0.7 0.0 copy-start.5
  0.7 0.0 copy-start.11
  0.7 1.1 %pack.1 = bf16[8,4224]{1,0:T(8,128)(2,1)S(1)} custom-call(bf16[8,2,2048]{2,1,0:T(2,128)(2,1)} %particles_hbm.1, s32[2,8]{1,0:T(2,128)} %offsets_hbm.1), custom_call_target="tpu_custom_call" | custom-call | tf_op jit(solution)/shard_map/pack/pallas_call | solution.py:193
  1.8 4.1 %collective-permute-start = (bf16[8,4224]{1,0:T(8,128)(2,1)S(1)}, bf16[8,4224]{1,0:T(8,128)(2,1)S(1)}, u32[]{:S(2)}, u32[]{:S(2)}) collective-permute-start(bf16[8,4224]{1,0:T(8,128)(2,1)S(1)} %pack.1), channel_id=1, source_target_pairs={{0,8},{1,9},{2,10},{3,11},{4,12},{5,13},{6,14},{7,15},{8,0},{9,1},... | collective-permute-start | bytes 202760 | tf_op jit(solution)/shard_map/ppermute | solution.py:510
  5.9 3.7 %collective-permute-done = bf16[8,4224]{1,0:T(8,128)(2,1)S(1)} collective-permute-done((bf16[8,4224]{1,0:T(8,128)(2,1)S(1)}, bf16[8,4224]{1,0:T(8,128)(2,1)S(1)}, u32[]{:S(2)}, u32[]{:S(2)}) %collective-permute-start) | collective-permute-done | bytes 67616 | tf_op jit(solution)/shard_map/ppermute | solution.py:510
  9.6 0.7 %collective-permute-start.1 = (bf16[16,4224]{1,0:T(8,128)(2,1)S(1)}, bf16[16,4224]{1,0:T(8,128)(2,1)S(1)}, u32[]{:S(2)}, u32[]{:S(2)}) collective-permute-start(bf16[16,4224]{1,0:T(8,128)(2,1)S(1)} %pad_maximum_fusion.2), channel_id=1, source_target_pairs={{0,4},{1,5},{2,6},{3,7},{4,0},{5,1},{6,2},{7,3},{8,12},{9,13},{10,... | collective-permute-start | bytes 405512 | tf_op jit(solution)/shard_map/ppermute | solution.py:510
  10.3 4.4 %collective-permute-done.1 = bf16[16,4224]{1,0:T(8,128)(2,1)S(1)} collective-permute-done((bf16[16,4224]{1,0:T(8,128)(2,1)S(1)}, bf16[16,4224]{1,0:T(8,128)(2,1)S(1)}, u32[]{:S(2)}, u32[]{:S(2)}) %collective-permute-start.1) | collective-permute-done | bytes 135200 | tf_op jit(solution)/shard_map/ppermute | solution.py:510
  14.7 1.8 %collective-permute-start.2 = (bf16[32,4224]{1,0:T(8,128)(2,1)S(1)}, bf16[32,4224]{1,0:T(8,128)(2,1)S(1)}, u32[]{:S(2)}, u32[]{:S(2)}) collective-permute-start(bf16[32,4224]{1,0:T(8,128)(2,1)S(1)} %pad_maximum_fusion.1), channel_id=1, source_target_pairs={{0,2},{1,3},{2,0},{3,1},{4,6},{5,7},{6,4},{7,5},{8,10},{9,11},{10,... | collective-permute-start | bytes 811016 | tf_op jit(solution)/shard_map/ppermute | solution.py:506
  16.5 0.9 %reshape.13 = bf16[4,2,32,64]{3,2,1,0:T(8,128)(2,1)S(1)} reshape(bf16[4,2,2048]{2,1,0:T(2,128)(2,1)} %param.17) | data formatting | bytes 65536 | tf_op jit(solution)/shard_map/reshape | solution.py:141
  17.4 0.1 copy.19
  17.5 0.1 reshape.14.refs_ref
  17.6 0.0 copy-done.8
  17.6 0.0 copy-done.9
  17.6 0.0 copy-done.5
  17.6 0.0 copy-done.11
  17.6 0.0 copy-start.1
  17.6 0.0 copy-start.2
  17.6 2.3 %rotated_spectra.1.bt_ref = bf16[512,4096]{1,0:T(8,128)(2,1)S(1)} custom-call(f32[32]{0:T(128)S(1)} %copy-done.11, bf16[128,128]{1,0:T(8,128)(2,1)S(1)} %reshape.14.refs_ref, bf16[128,384]{1,0:T(8,128)(2,1)S(1)} %copy-done.5, f32[64,128]{1,0:T(8,128)S(1)} %copy-done.9, f32[64,128]{1,0:T(8,128)S(1)} %copy-done.8), custom_call_target="tpu_custom_call" | custom-call | flops 16777216 | bytes 4194304 | tf_op jit(solution)/shard_map/rotated_spectra/pallas_call | solution.py:147
  19.9 0.0 copy-start
  20.0 0.0 copy-start.4
  20.0 0.0 copy-start.10
  20.0 1.3 %collective-permute-done.2 = bf16[32,4224]{1,0:T(8,128)(2,1)S(1)} collective-permute-done((bf16[32,4224]{1,0:T(8,128)(2,1)S(1)}, bf16[32,4224]{1,0:T(8,128)(2,1)S(1)}, u32[]{:S(2)}, u32[]{:S(2)}) %collective-permute-start.2) | collective-permute-done | bytes 270368 | tf_op jit(solution)/shard_map/ppermute | solution.py:506
  21.3 0.0 copy-start.3
  21.3 0.0 copy-start.6
  21.3 0.0 copy-start.7
  21.4 0.1 collective-permute-start.3
  21.4 1.9 %collective-permute-done.3.far_ref = bf16[64,4224]{1,0:T(8,128)(2,1)S(1)} collective-permute-done((bf16[64,4224]{1,0:T(8,128)(2,1)S(1)}, bf16[64,4224]{1,0:T(8,128)(2,1)S(1)}, u32[]{:S(2)}, u32[]{:S(2)}) %collective-permute-start.3) | collective-permute-done | bytes 540704 | tf_op jit(solution)/shard_map/ppermute | solution.py:510
  23.4 0.0 copy-done.1
  23.4 0.0 copy-done.2
  23.4 0.0 copy-done
  23.4 0.0 copy-done.4
  23.4 0.0 copy-done.10
  23.4 18.4 %local_scores.1 = (bf16[1200,4096]{1,0:T(8,128)(2,1)S(1)}, f32[1200,256]{1,0:T(8,128)S(1)}, f32[16,1,8,128]{3,2,1,0:T(8,128)S(1)}) custom-call(s32[16]{0:T(128)S(1)} %copy-done.10, bf16[64,4224]{1,0:T(8,128)(2,1)S(1)} %pad_maximum_fusion.near_ref, bf16[64,4224]{1,0:T(8,128)(2,1)S(1)} %collective-permute-done.3.far_ref, bf16[96,4096]{1,0:T(8,128)(2,1)S(1)} %copy-done, ...), custom_call_target="tpu_custom_call" | custom-call | tf_op jit(solution)/shard_map/local_scores/pallas_call | solution.py:344
  41.7 13.3 %all_to_all.5.stats_ref = f32[16,1,8,128]{3,2,1,0:T(8,128)S(1)} all-to-all(f32[16,1,8,128]{3,2,1,0:T(8,128)S(1)} %get-tuple-element.11), channel_id=1, replica_groups=mesh['parts'=2,'blk'=16] {'blk'}, dimensions={0} | all-to-all | bytes 131072 | tf_op jit(solution)/shard_map/all_to_all | solution.py:516
  55.1 0.0 copy-done.3
  55.1 0.0 copy-done.6
  55.1 0.0 copy-done.7
  55.1 7.5 %local_sums.1 = (f32[1,8]{1,0:T(1,128)}, f32[4,2,2048]{2,1,0:T(2,128)}) custom-call(s32[16]{0:T(128)S(1)} %copy-done.10, f32[16,1,8,128]{3,2,1,0:T(8,128)S(1)} %all_to_all.5.stats_ref, f32[1200,256]{1,0:T(8,128)S(1)} %get-tuple-element.12.expo_ref, bf16[1200,4096]{1,0:T(8,128)(2,1)S(1)} %get-tuple-element.13.hat_ref, f32[64,256]{1,0:T(8,128)S(1)} %copy-done.7, ...), custom_call_target="tpu_custom_call" | custom-call | tf_op jit(solution)/shard_map/local_sums/pallas_call | solution.py:478
  (3 shorter events, 0.1 us)
Async XLA Ops:
  0.6 16.9 %copy-start.8 = (f32[64,128]{1,0:T(8,128)S(1)}, f32[64,128]{1,0:T(8,128)}, u32[]{:S(2)}) copy-start(f32[64,128]{1,0:T(8,128)} %constant.22.clone.sin_ref) | copy-start | bytes 98308
  0.6 16.9 %copy-start.9 = (f32[64,128]{1,0:T(8,128)S(1)}, f32[64,128]{1,0:T(8,128)}, u32[]{:S(2)}) copy-start(f32[64,128]{1,0:T(8,128)} %constant.21.clone.cos_ref) | copy-start | bytes 98308
  0.7 16.9 %copy-start.5 = (bf16[128,384]{1,0:T(8,128)(2,1)S(1)}, bf16[128,384]{1,0:T(8,128)(2,1)}, u32[]{:S(2)}) copy-start(bf16[128,384]{1,0:T(8,128)(2,1)} %constant.20.clone.trio_ref) | copy-start | bytes 294916
  0.7 16.9 %copy-start.11 = (f32[32]{0:T(128)S(1)}, f32[32]{0:T(128)}, u32[]{:S(2)}) copy-start(f32[32]{0:T(128)} %noise_ref.1) | copy-start | bytes 388
  1.8 7.8 %collective-permute-start = (bf16[8,4224]{1,0:T(8,128)(2,1)S(1)}, bf16[8,4224]{1,0:T(8,128)(2,1)S(1)}, u32[]{:S(2)}, u32[]{:S(2)}) collective-permute-start(bf16[8,4224]{1,0:T(8,128)(2,1)S(1)} %pack.1), channel_id=1, source_target_pairs={{0,8},{1,9},{2,10},{3,11},{4,12},{5,13},{6,14},{7,15},{8,0},{9,1},... | collective-permute-start | bytes 202760 | tf_op jit(solution)/shard_map/ppermute | solution.py:510
  9.6 5.1 %collective-permute-start.1 = (bf16[16,4224]{1,0:T(8,128)(2,1)S(1)}, bf16[16,4224]{1,0:T(8,128)(2,1)S(1)}, u32[]{:S(2)}, u32[]{:S(2)}) collective-permute-start(bf16[16,4224]{1,0:T(8,128)(2,1)S(1)} %pad_maximum_fusion.2), channel_id=1, source_target_pairs={{0,4},{1,5},{2,6},{3,7},{4,0},{5,1},{6,2},{7,3},{8,12},{9,13},{10,... | collective-permute-start | bytes 405512 | tf_op jit(solution)/shard_map/ppermute | solution.py:510
  14.7 6.5 %collective-permute-start.2 = (bf16[32,4224]{1,0:T(8,128)(2,1)S(1)}, bf16[32,4224]{1,0:T(8,128)(2,1)S(1)}, u32[]{:S(2)}, u32[]{:S(2)}) collective-permute-start(bf16[32,4224]{1,0:T(8,128)(2,1)S(1)} %pad_maximum_fusion.1), channel_id=1, source_target_pairs={{0,2},{1,3},{2,0},{3,1},{4,6},{5,7},{6,4},{7,5},{8,10},{9,11},{10,... | collective-permute-start | bytes 811016 | tf_op jit(solution)/shard_map/ppermute | solution.py:506
  17.6 5.8 %copy-start.1 = (f32[25,4096]{1,0:T(8,128)S(1)}, f32[25,4096]{1,0:T(8,128)}, u32[]{:S(2)}) copy-start(f32[25,4096]{1,0:T(8,128)} %constant.25.clone.ts_ref) | copy-start | bytes 1228804
  17.6 5.7 %copy-start.2 = (f32[25,4096]{1,0:T(8,128)S(1)}, f32[25,4096]{1,0:T(8,128)}, u32[]{:S(2)}) copy-start(f32[25,4096]{1,0:T(8,128)} %constant.24.clone.tc_ref) | copy-start | bytes 1228804
  19.9 3.4 %copy-start = (bf16[96,4096]{1,0:T(8,128)(2,1)S(1)}, bf16[96,4096]{1,0:T(8,128)(2,1)}, u32[]{:S(2)}) copy-start(bf16[96,4096]{1,0:T(8,128)(2,1)} %constant.23.clone.offset_ref) | copy-start | bytes 2359300
  20.0 3.4 %copy-start.4 = (bf16[256,256]{1,0:T(8,128)(2,1)S(1)}, bf16[256,256]{1,0:T(8,128)(2,1)}, u32[]{:S(2)}) copy-start(bf16[256,256]{1,0:T(8,128)(2,1)} %constant.26.clone.forward_ref) | copy-start | bytes 393220
  20.0 3.4 %copy-start.10 = (s32[16]{0:T(128)S(1)}, s32[16]{0:T(128)}, u32[]{:S(2)}) copy-start(s32[16]{0:T(128)} %counts_ref.3) | copy-start | bytes 196
  21.3 33.8 %copy-start.3 = (bf16[256,512]{1,0:T(8,128)(2,1)S(1)}, bf16[256,512]{1,0:T(8,128)(2,1)}, u32[]{:S(2)}) copy-start(bf16[256,512]{1,0:T(8,128)(2,1)} %constant.29.clone.image_ref) | copy-start | bytes 786436
  21.3 33.8 %copy-start.6 = (f32[64,256]{1,0:T(8,128)S(1)}, f32[64,256]{1,0:T(8,128)}, u32[]{:S(2)}) copy-start(f32[64,256]{1,0:T(8,128)} %constant.28.clone.sin_ref) | copy-start | bytes 196612
  21.3 33.7 %copy-start.7 = (f32[64,256]{1,0:T(8,128)S(1)}, f32[64,256]{1,0:T(8,128)}, u32[]{:S(2)}) copy-start(f32[64,256]{1,0:T(8,128)} %constant.27.clone.cos_ref) | copy-start | bytes 196612
  21.4 2.0 %collective-permute-start.3 = (bf16[64,4224]{1,0:T(8,128)(2,1)S(1)}, bf16[64,4224]{1,0:T(8,128)(2,1)S(1)}, u32[]{:S(2)}, u32[]{:S(2)}) collective-permute-start(bf16[64,4224]{1,0:T(8,128)(2,1)S(1)} %pad_maximum_fusion.near_ref), channel_id=1, source_target_pairs={{0,1},{1,0},{2,3},{3,2},{4,5},{5,4},{6,7},{7,6},{8,9},{9,8},{10,11... | collective-permute-start | bytes 1622024 | tf_op jit(solution)/shard_map/ppermute | solution.py:510

commit v2 on v1

--- a/solution.py
+++ b/solution.py
@@ -391,8 +391,7 @@
 
     def weigh(value, width, at):
         high, low = halves(value.T)
-        weight_ref[:columns, at : at + width] = high[:, :width]
-        weight_ref[columns:, at : at + width] = low[:, :width]
+        weight_ref[:, at : at + width] = high[:, :width]
 
     for block in range(ROWS // 384):
         value = expo_ref[block * 384 : (block + 1) * 384, :] * repeated
@@ -411,7 +410,7 @@
     def body(i, carry):
         lanes = pl.ds(pl.multiple_of(i * (WIDE * PAIR), WIDE * PAIR), WIDE * PAIR)
         both = dot(weight_ref[...], hat_ref[:, lanes])
-        totals = both[:columns] + both[columns:]
+        totals = both
         for q in range(WIDE):
             turn_back(i * WIDE + q, totals[:, q * PAIR : (q + 1) * PAIR])
         return carry
@@ -484,7 +483,7 @@
         in_specs=[pl.BlockSpec(memory_space=pltpu.SMEM), vmem, place, place, vmem, vmem, vmem],
         out_specs=(vmem, vmem),
         scratch_shapes=[
-            pltpu.VMEM((2 * columns, ROWS), BF16),
+            pltpu.VMEM((columns, ROWS), BF16),
             pltpu.VMEM((pairs, -(-classes // 8) * 8, PAIR), F32),
             *spare,
         ],

time: 62.9 us -> 60.2 us (0.957)
  Pallas kernels: 29.3 us -> 26.6 us
    pallas_call x1, Pallas kernels: 7.51 us -> 4.85 us  [local_sums(): pl.pallas_call(functools.partial(sum_kernel, classes, chunks), out_shape=...]
where the time goes in v2:
time: 60.2 us; the launch traced here: 59.9 us
  Pallas kernels  26.6 us (44%)
  blocking collectives  13.3 us (22%)
  waiting for transfers between devices  11.3 us (19%)
  starting transfers between devices  6.62 us (11%)
  local copies, waits for them, and re-layouts  1.1 us (2%)
  between operations  0.83 us (1%)
    pallas_call x1, Pallas kernels, local_scores(): pl.pallas_call(functools.partial(score_kernel, cycles, slots, chunks), ou...  18.4 us
    all_to_all x1, blocking collectives, local(): stats = lax.all_to_all(stats, 'blk', 0, 0, tiled=True)  13.3 us
    ppermute x4, waiting for transfers between devices, local(): lax.ppermute(packed, 'blk', [(i, i ^ distance) for i in range(devices)])  11.3 us
    ppermute x4, starting transfers between devices, local(): lax.ppermute(packed, 'blk', [(i, i ^ distance) for i in range(devices)])  6.62 us
    pallas_call x1, Pallas kernels, local_sums(): pl.pallas_call(functools.partial(sum_kernel, classes, chunks), out_shape=...  4.85 us
    pallas_call x1, Pallas kernels, rotated_spectra(): pl.pallas_call(functools.partial(spectra_kernel, cycles), out_shape=pltpu...  2.31 us
  transfers between devices with their start and end apart: 4, of which 4 were waited for; matrix products, arithmetic and copies ran while one was open for 2% of the time, Pallas kernels for 4%

profile of v2, /device:TPU:0, one launch (start us, length us, event | category | flops | bytes accessed | tf_op | source)
XLA Modules:
  0.0 59.9 jit_solution(15999466195464503272)
XLA Ops:
  0.6 0.0 copy-start.8
  0.6 0.0 copy-start.9
  0.7 0.0 copy-start.5
  0.7 0.0 copy-start.11
  0.7 1.1 %pack.1 = bf16[8,4224]{1,0:T(8,128)(2,1)S(1)} custom-call(bf16[8,2,2048]{2,1,0:T(2,128)(2,1)} %particles_hbm.1, s32[2,8]{1,0:T(2,128)} %offsets_hbm.1), custom_call_target="tpu_custom_call" | custom-call | tf_op jit(solution)/shard_map/pack/pallas_call | solution.py:193
  1.8 4.1 %collective-permute-start = (bf16[8,4224]{1,0:T(8,128)(2,1)S(1)}, bf16[8,4224]{1,0:T(8,128)(2,1)S(1)}, u32[]{:S(2)}, u32[]{:S(2)}) collective-permute-start(bf16[8,4224]{1,0:T(8,128)(2,1)S(1)} %pack.1), channel_id=1, source_target_pairs={{0,8},{1,9},{2,10},{3,11},{4,12},{5,13},{6,14},{7,15},{8,0},{9,1},... | collective-permute-start | bytes 202760 | tf_op jit(solution)/shard_map/ppermute | solution.py:509
  5.9 3.7 %collective-permute-done = bf16[8,4224]{1,0:T(8,128)(2,1)S(1)} collective-permute-done((bf16[8,4224]{1,0:T(8,128)(2,1)S(1)}, bf16[8,4224]{1,0:T(8,128)(2,1)S(1)}, u32[]{:S(2)}, u32[]{:S(2)}) %collective-permute-start) | collective-permute-done | bytes 67616 | tf_op jit(solution)/shard_map/ppermute | solution.py:509
  9.6 0.7 %collective-permute-start.1 = (bf16[16,4224]{1,0:T(8,128)(2,1)S(1)}, bf16[16,4224]{1,0:T(8,128)(2,1)S(1)}, u32[]{:S(2)}, u32[]{:S(2)}) collective-permute-start(bf16[16,4224]{1,0:T(8,128)(2,1)S(1)} %pad_maximum_fusion.2), channel_id=1, source_target_pairs={{0,4},{1,5},{2,6},{3,7},{4,0},{5,1},{6,2},{7,3},{8,12},{9,13},{10,... | collective-permute-start | bytes 405512 | tf_op jit(solution)/shard_map/ppermute | solution.py:509
  10.3 4.4 %collective-permute-done.1 = bf16[16,4224]{1,0:T(8,128)(2,1)S(1)} collective-permute-done((bf16[16,4224]{1,0:T(8,128)(2,1)S(1)}, bf16[16,4224]{1,0:T(8,128)(2,1)S(1)}, u32[]{:S(2)}, u32[]{:S(2)}) %collective-permute-start.1) | collective-permute-done | bytes 135200 | tf_op jit(solution)/shard_map/ppermute | solution.py:509
  14.7 1.8 %collective-permute-start.2 = (bf16[32,4224]{1,0:T(8,128)(2,1)S(1)}, bf16[32,4224]{1,0:T(8,128)(2,1)S(1)}, u32[]{:S(2)}, u32[]{:S(2)}) collective-permute-start(bf16[32,4224]{1,0:T(8,128)(2,1)S(1)} %pad_maximum_fusion.1), channel_id=1, source_target_pairs={{0,2},{1,3},{2,0},{3,1},{4,6},{5,7},{6,4},{7,5},{8,10},{9,11},{10,... | collective-permute-start | bytes 811016 | tf_op jit(solution)/shard_map/ppermute | solution.py:505
  16.5 0.9 %reshape.13 = bf16[4,2,32,64]{3,2,1,0:T(8,128)(2,1)S(1)} reshape(bf16[4,2,2048]{2,1,0:T(2,128)(2,1)} %param.17) | data formatting | bytes 65536 | tf_op jit(solution)/shard_map/reshape | solution.py:141
  17.4 0.1 copy.19
  17.5 0.1 reshape.14.refs_ref
  17.6 0.0 copy-done.8
  17.6 0.0 copy-done.9
  17.6 0.0 copy-done.5
  17.6 0.0 copy-done.11
  17.6 0.0 copy-start.1
  17.6 0.0 copy-start.2
  17.6 2.3 %rotated_spectra.1.bt_ref = bf16[512,4096]{1,0:T(8,128)(2,1)S(1)} custom-call(f32[32]{0:T(128)S(1)} %copy-done.11, bf16[128,128]{1,0:T(8,128)(2,1)S(1)} %reshape.14.refs_ref, bf16[128,384]{1,0:T(8,128)(2,1)S(1)} %copy-done.5, f32[64,128]{1,0:T(8,128)S(1)} %copy-done.9, f32[64,128]{1,0:T(8,128)S(1)} %copy-done.8), custom_call_target="tpu_custom_call" | custom-call | flops 16777216 | bytes 4194304 | tf_op jit(solution)/shard_map/rotated_spectra/pallas_call | solution.py:147
  19.9 0.0 copy-start
  20.0 0.0 copy-start.4
  20.0 0.0 copy-start.10
  20.0 1.3 %collective-permute-done.2 = bf16[32,4224]{1,0:T(8,128)(2,1)S(1)} collective-permute-done((bf16[32,4224]{1,0:T(8,128)(2,1)S(1)}, bf16[32,4224]{1,0:T(8,128)(2,1)S(1)}, u32[]{:S(2)}, u32[]{:S(2)}) %collective-permute-start.2) | collective-permute-done | bytes 270368 | tf_op jit(solution)/shard_map/ppermute | solution.py:505
  21.3 0.0 copy-start.3
  21.3 0.0 copy-start.6
  21.3 0.0 copy-start.7
  21.4 0.1 collective-permute-start.3
  21.4 1.9 %collective-permute-done.3.far_ref = bf16[64,4224]{1,0:T(8,128)(2,1)S(1)} collective-permute-done((bf16[64,4224]{1,0:T(8,128)(2,1)S(1)}, bf16[64,4224]{1,0:T(8,128)(2,1)S(1)}, u32[]{:S(2)}, u32[]{:S(2)}) %collective-permute-start.3) | collective-permute-done | bytes 540704 | tf_op jit(solution)/shard_map/ppermute | solution.py:509
  23.4 0.0 copy-done.1
  23.4 0.0 copy-done.2
  23.4 0.0 copy-done
  23.4 0.0 copy-done.4
  23.4 0.0 copy-done.10
  23.4 18.4 %local_scores.1 = (bf16[1200,4096]{1,0:T(8,128)(2,1)S(1)}, f32[1200,256]{1,0:T(8,128)S(1)}, f32[16,1,8,128]{3,2,1,0:T(8,128)S(1)}) custom-call(s32[16]{0:T(128)S(1)} %copy-done.10, bf16[64,4224]{1,0:T(8,128)(2,1)S(1)} %pad_maximum_fusion.near_ref, bf16[64,4224]{1,0:T(8,128)(2,1)S(1)} %collective-permute-done.3.far_ref, bf16[96,4096]{1,0:T(8,128)(2,1)S(1)} %copy-done, ...), custom_call_target="tpu_custom_call" | custom-call | tf_op jit(solution)/shard_map/local_scores/pallas_call | solution.py:344
  41.7 13.3 %all_to_all.5.stats_ref = f32[16,1,8,128]{3,2,1,0:T(8,128)S(1)} all-to-all(f32[16,1,8,128]{3,2,1,0:T(8,128)S(1)} %get-tuple-element.11), channel_id=1, replica_groups=mesh['parts'=2,'blk'=16] {'blk'}, dimensions={0} | all-to-all | bytes 131072 | tf_op jit(solution)/shard_map/all_to_all | solution.py:515
  55.1 0.0 copy-done.3
  55.1 0.0 copy-done.6
  55.1 0.0 copy-done.7
  55.1 4.9 %local_sums.1 = (f32[1,8]{1,0:T(1,128)}, f32[4,2,2048]{2,1,0:T(2,128)}) custom-call(s32[16]{0:T(128)S(1)} %copy-done.10, f32[16,1,8,128]{3,2,1,0:T(8,128)S(1)} %all_to_all.5.stats_ref, f32[1200,256]{1,0:T(8,128)S(1)} %get-tuple-element.12.expo_ref, bf16[1200,4096]{1,0:T(8,128)(2,1)S(1)} %get-tuple-element.13.hat_ref, f32[64,256]{1,0:T(8,128)S(1)} %copy-done.7, ...), custom_call_target="tpu_custom_call" | custom-call | tf_op jit(solution)/shard_map/local_sums/pallas_call | solution.py:477
  (3 shorter events, 0.1 us)
Async XLA Ops:
  0.6 16.9 %copy-start.8 = (f32[64,128]{1,0:T(8,128)S(1)}, f32[64,128]{1,0:T(8,128)}, u32[]{:S(2)}) copy-start(f32[64,128]{1,0:T(8,128)} %constant.22.clone.sin_ref) | copy-start | bytes 98308
  0.6 16.9 %copy-start.9 = (f32[64,128]{1,0:T(8,128)S(1)}, f32[64,128]{1,0:T(8,128)}, u32[]{:S(2)}) copy-start(f32[64,128]{1,0:T(8,128)} %constant.21.clone.cos_ref) | copy-start | bytes 98308
  0.7 16.9 %copy-start.5 = (bf16[128,384]{1,0:T(8,128)(2,1)S(1)}, bf16[128,384]{1,0:T(8,128)(2,1)}, u32[]{:S(2)}) copy-start(bf16[128,384]{1,0:T(8,128)(2,1)} %constant.20.clone.trio_ref) | copy-start | bytes 294916
  0.7 16.9 %copy-start.11 = (f32[32]{0:T(128)S(1)}, f32[32]{0:T(128)}, u32[]{:S(2)}) copy-start(f32[32]{0:T(128)} %noise_ref.1) | copy-start | bytes 388
  1.8 7.8 %collective-permute-start = (bf16[8,4224]{1,0:T(8,128)(2,1)S(1)}, bf16[8,4224]{1,0:T(8,128)(2,1)S(1)}, u32[]{:S(2)}, u32[]{:S(2)}) collective-permute-start(bf16[8,4224]{1,0:T(8,128)(2,1)S(1)} %pack.1), channel_id=1, source_target_pairs={{0,8},{1,9},{2,10},{3,11},{4,12},{5,13},{6,14},{7,15},{8,0},{9,1},... | collective-permute-start | bytes 202760 | tf_op jit(solution)/shard_map/ppermute | solution.py:509
  9.6 5.1 %collective-permute-start.1 = (bf16[16,4224]{1,0:T(8,128)(2,1)S(1)}, bf16[16,4224]{1,0:T(8,128)(2,1)S(1)}, u32[]{:S(2)}, u32[]{:S(2)}) collective-permute-start(bf16[16,4224]{1,0:T(8,128)(2,1)S(1)} %pad_maximum_fusion.2), channel_id=1, source_target_pairs={{0,4},{1,5},{2,6},{3,7},{4,0},{5,1},{6,2},{7,3},{8,12},{9,13},{10,... | collective-permute-start | bytes 405512 | tf_op jit(solution)/shard_map/ppermute | solution.py:509
  14.7 6.5 %collective-permute-start.2 = (bf16[32,4224]{1,0:T(8,128)(2,1)S(1)}, bf16[32,4224]{1,0:T(8,128)(2,1)S(1)}, u32[]{:S(2)}, u32[]{:S(2)}) collective-permute-start(bf16[32,4224]{1,0:T(8,128)(2,1)S(1)} %pad_maximum_fusion.1), channel_id=1, source_target_pairs={{0,2},{1,3},{2,0},{3,1},{4,6},{5,7},{6,4},{7,5},{8,10},{9,11},{10,... | collective-permute-start | bytes 811016 | tf_op jit(solution)/shard_map/ppermute | solution.py:505
  17.6 5.8 %copy-start.1 = (f32[25,4096]{1,0:T(8,128)S(1)}, f32[25,4096]{1,0:T(8,128)}, u32[]{:S(2)}) copy-start(f32[25,4096]{1,0:T(8,128)} %constant.25.clone.ts_ref) | copy-start | bytes 1228804
  17.6 5.7 %copy-start.2 = (f32[25,4096]{1,0:T(8,128)S(1)}, f32[25,4096]{1,0:T(8,128)}, u32[]{:S(2)}) copy-start(f32[25,4096]{1,0:T(8,128)} %constant.24.clone.tc_ref) | copy-start | bytes 1228804
  19.9 3.4 %copy-start = (bf16[96,4096]{1,0:T(8,128)(2,1)S(1)}, bf16[96,4096]{1,0:T(8,128)(2,1)}, u32[]{:S(2)}) copy-start(bf16[96,4096]{1,0:T(8,128)(2,1)} %constant.23.clone.offset_ref) | copy-start | bytes 2359300
  20.0 3.4 %copy-start.4 = (bf16[256,256]{1,0:T(8,128)(2,1)S(1)}, bf16[256,256]{1,0:T(8,128)(2,1)}, u32[]{:S(2)}) copy-start(bf16[256,256]{1,0:T(8,128)(2,1)} %constant.26.clone.forward_ref) | copy-start | bytes 393220
  20.0 3.4 %copy-start.10 = (s32[16]{0:T(128)S(1)}, s32[16]{0:T(128)}, u32[]{:S(2)}) copy-start(s32[16]{0:T(128)} %counts_ref.3) | copy-start | bytes 196
  21.3 33.8 %copy-start.3 = (bf16[256,512]{1,0:T(8,128)(2,1)S(1)}, bf16[256,512]{1,0:T(8,128)(2,1)}, u32[]{:S(2)}) copy-start(bf16[256,512]{1,0:T(8,128)(2,1)} %constant.29.clone.image_ref) | copy-start | bytes 786436
  21.3 33.8 %copy-start.6 = (f32[64,256]{1,0:T(8,128)S(1)}, f32[64,256]{1,0:T(8,128)}, u32[]{:S(2)}) copy-start(f32[64,256]{1,0:T(8,128)} %constant.28.clone.sin_ref) | copy-start | bytes 196612
  21.3 33.7 %copy-start.7 = (f32[64,256]{1,0:T(8,128)S(1)}, f32[64,256]{1,0:T(8,128)}, u32[]{:S(2)}) copy-start(f32[64,256]{1,0:T(8,128)} %constant.27.clone.cos_ref) | copy-start | bytes 196612
  21.4 2.0 %collective-permute-start.3 = (bf16[64,4224]{1,0:T(8,128)(2,1)S(1)}, bf16[64,4224]{1,0:T(8,128)(2,1)S(1)}, u32[]{:S(2)}, u32[]{:S(2)}) collective-permute-start(bf16[64,4224]{1,0:T(8,128)(2,1)S(1)} %pad_maximum_fusion.near_ref), channel_id=1, source_target_pairs={{0,1},{1,0},{2,3},{3,2},{4,5},{5,4},{6,7},{7,6},{8,9},{9,8},{10,11... | collective-permute-start | bytes 1622024 | tf_op jit(solution)/shard_map/ppermute | solution.py:509

commit v3 on v2

--- a/solution.py
+++ b/solution.py
@@ -17,7 +17,7 @@
 ROWS = STEPS * CHUNK
 PAIR = 4 * ANGLES
 WIDE = 16
-STEP_GROUPS = tuple(tuple(g) for g in (range(i, min(i + 9, STEPS)) for i in range(0, STEPS, 9)))
+STEP_GROUPS = ((0, 1, 2, 3, 4, 5, 6, 7, 8), (9, 10, 11, 12))
 F32 = jnp.float32
 BF16 = jnp.bfloat16
 MIB = 1024 * 1024
@@ -261,20 +261,32 @@
     def transform(jp, carry):
         lanes = pl.ds(pl.multiple_of(jp * PAIR, PAIR), PAIR)
         plain, swapped = plain_ref[jp], swap_ref[jp]
+        base = 0
         for steps in STEP_GROUPS:
-            for t in steps:
-                y = plain * tc_ref[t : t + 1, lanes] + swapped * ts_ref[t : t + 1, lanes]
-                high, low = halves(y)
-                rows = slice(t * CHUNK, (t + 1) * CHUNK)
+            pieces = [(plain, tc_ref, t) for t in steps]
+            pieces += [(swapped, ts_ref, t) for t in steps if t != STEPS // 2]
+            for i, (value, table_ref, t) in enumerate(pieces):
+                high, low = halves(value * table_ref[t : t + 1, lanes])
+                rows = slice(base + i * CHUNK, base + (i + 1) * CHUNK)
                 stack_ref[0, rows, :128] = high[:, :128]
                 stack_ref[0, rows, 128:] = low[:, :128]
                 stack_ref[1, rows, :128] = high[:, 128:]
                 stack_ref[1, rows, 128:] = low[:, 128:]
-            rows = slice(steps[0] * CHUNK, (steps[-1] + 1) * CHUNK)
             for parity in range(2):
-                both = dot(stack_ref[parity, rows], forward_ref[...])
+                both = dot(stack_ref[parity, base : base + len(pieces) * CHUNK], forward_ref[...])
+                whole = both[:, :128] + both[:, 128:]
                 columns = pl.ds(pl.multiple_of(jp * PAIR + parity * 128, 128), 128)
-                hat_ref[rows, columns] = (both[:, :128] + both[:, 128:]).astype(BF16)
+                for i, t in enumerate(steps):
+                    even = whole[i * CHUNK : (i + 1) * CHUNK]
+                    mirror = STEPS - 1 - t
+                    if mirror == t:
+                        hat_ref[t * CHUNK : (t + 1) * CHUNK, columns] = even.astype(BF16)
+                        continue
+                    at = (len(steps) + i) * CHUNK
+                    odd = whole[at : at + CHUNK]
+                    hat_ref[t * CHUNK : (t + 1) * CHUNK, columns] = (even + odd).astype(BF16)
+                    hat_ref[mirror * CHUNK : (mirror + 1) * CHUNK, columns] = (even - odd).astype(BF16)
+            base += len(pieces) * CHUNK
         return carry
 
     lax.fori_loop(0, cycles // 2, transform, 0)

time: 60.2 us -> 58 us (0.963)
  Pallas kernels: 26.6 us -> 24.4 us
    pallas_call x1, Pallas kernels: 18.4 us -> 16.1 us  [local_scores(): pl.pallas_call(functools.partial(score_kernel, cycles, slots, chunks), ou...]
where the time goes in v3:
time: 58 us; the launch traced here: 57.7 us
  Pallas kernels  24.4 us (42%)
  blocking collectives  13.3 us (23%)
  waiting for transfers between devices  11.3 us (19%)
  starting transfers between devices  6.62 us (11%)
  local copies, waits for them, and re-layouts  1.1 us (2%)
  between operations  0.83 us (1%)
    pallas_call x1, Pallas kernels, local_scores(): pl.pallas_call(functools.partial(score_kernel, cycles, slots, chunks), ou...  16.1 us
    all_to_all x1, blocking collectives, local(): stats = lax.all_to_all(stats, 'blk', 0, 0, tiled=True)  13.3 us
    ppermute x4, waiting for transfers between devices, local(): lax.ppermute(packed, 'blk', [(i, i ^ distance) for i in range(devices)])  11.3 us
    ppermute x4, starting transfers between devices, local(): lax.ppermute(packed, 'blk', [(i, i ^ distance) for i in range(devices)])  6.62 us
    pallas_call x1, Pallas kernels, local_sums(): pl.pallas_call(functools.partial(sum_kernel, classes, chunks), out_shape=...  4.85 us
    pallas_call x1, Pallas kernels, rotated_spectra(): pl.pallas_call(functools.partial(spectra_kernel, cycles), out_shape=pltpu...  2.31 us
  transfers between devices with their start and end apart: 4, of which 4 were waited for; matrix products, arithmetic and copies ran while one was open for 2% of the time, Pallas kernels for 4%

profile of v3, /device:TPU:0, one launch (start us, length us, event | category | flops | bytes accessed | tf_op | source)
XLA Modules:
  0.0 57.7 jit_solution(11598343085358663105)
XLA Ops:
  0.6 0.0 copy-start.8
  0.6 0.0 copy-start.9
  0.7 0.0 copy-start.5
  0.7 0.0 copy-start.11
  0.7 1.1 %pack.1 = bf16[8,4224]{1,0:T(8,128)(2,1)S(1)} custom-call(bf16[8,2,2048]{2,1,0:T(2,128)(2,1)} %particles_hbm.1, s32[2,8]{1,0:T(2,128)} %offsets_hbm.1), custom_call_target="tpu_custom_call" | custom-call | tf_op jit(solution)/shard_map/pack/pallas_call | solution.py:193
  1.8 4.1 %collective-permute-start = (bf16[8,4224]{1,0:T(8,128)(2,1)S(1)}, bf16[8,4224]{1,0:T(8,128)(2,1)S(1)}, u32[]{:S(2)}, u32[]{:S(2)}) collective-permute-start(bf16[8,4224]{1,0:T(8,128)(2,1)S(1)} %pack.1), channel_id=1, source_target_pairs={{0,8},{1,9},{2,10},{3,11},{4,12},{5,13},{6,14},{7,15},{8,0},{9,1},... | collective-permute-start | bytes 202760 | tf_op jit(solution)/shard_map/ppermute | solution.py:521
  5.9 3.7 %collective-permute-done = bf16[8,4224]{1,0:T(8,128)(2,1)S(1)} collective-permute-done((bf16[8,4224]{1,0:T(8,128)(2,1)S(1)}, bf16[8,4224]{1,0:T(8,128)(2,1)S(1)}, u32[]{:S(2)}, u32[]{:S(2)}) %collective-permute-start) | collective-permute-done | bytes 67616 | tf_op jit(solution)/shard_map/ppermute | solution.py:521
  9.6 0.7 %collective-permute-start.1 = (bf16[16,4224]{1,0:T(8,128)(2,1)S(1)}, bf16[16,4224]{1,0:T(8,128)(2,1)S(1)}, u32[]{:S(2)}, u32[]{:S(2)}) collective-permute-start(bf16[16,4224]{1,0:T(8,128)(2,1)S(1)} %pad_maximum_fusion.2), channel_id=1, source_target_pairs={{0,4},{1,5},{2,6},{3,7},{4,0},{5,1},{6,2},{7,3},{8,12},{9,13},{10,... | collective-permute-start | bytes 405512 | tf_op jit(solution)/shard_map/ppermute | solution.py:521
  10.3 4.4 %collective-permute-done.1 = bf16[16,4224]{1,0:T(8,128)(2,1)S(1)} collective-permute-done((bf16[16,4224]{1,0:T(8,128)(2,1)S(1)}, bf16[16,4224]{1,0:T(8,128)(2,1)S(1)}, u32[]{:S(2)}, u32[]{:S(2)}) %collective-permute-start.1) | collective-permute-done | bytes 135200 | tf_op jit(solution)/shard_map/ppermute | solution.py:521
  14.7 1.8 %collective-permute-start.2 = (bf16[32,4224]{1,0:T(8,128)(2,1)S(1)}, bf16[32,4224]{1,0:T(8,128)(2,1)S(1)}, u32[]{:S(2)}, u32[]{:S(2)}) collective-permute-start(bf16[32,4224]{1,0:T(8,128)(2,1)S(1)} %pad_maximum_fusion.1), channel_id=1, source_target_pairs={{0,2},{1,3},{2,0},{3,1},{4,6},{5,7},{6,4},{7,5},{8,10},{9,11},{10,... | collective-permute-start | bytes 811016 | tf_op jit(solution)/shard_map/ppermute | solution.py:517
  16.5 0.9 %reshape.13 = bf16[4,2,32,64]{3,2,1,0:T(8,128)(2,1)S(1)} reshape(bf16[4,2,2048]{2,1,0:T(2,128)(2,1)} %param.17) | data formatting | bytes 65536 | tf_op jit(solution)/shard_map/reshape | solution.py:141
  17.4 0.1 copy.19
  17.5 0.1 reshape.14.refs_ref
  17.6 0.0 copy-done.8
  17.6 0.0 copy-done.9
  17.6 0.0 copy-done.5
  17.6 0.0 copy-done.11
  17.6 0.0 copy-start.1
  17.6 0.0 copy-start.2
  17.6 2.3 %rotated_spectra.1.bt_ref = bf16[512,4096]{1,0:T(8,128)(2,1)S(1)} custom-call(f32[32]{0:T(128)S(1)} %copy-done.11, bf16[128,128]{1,0:T(8,128)(2,1)S(1)} %reshape.14.refs_ref, bf16[128,384]{1,0:T(8,128)(2,1)S(1)} %copy-done.5, f32[64,128]{1,0:T(8,128)S(1)} %copy-done.9, f32[64,128]{1,0:T(8,128)S(1)} %copy-done.8), custom_call_target="tpu_custom_call" | custom-call | flops 16777216 | bytes 4194304 | tf_op jit(solution)/shard_map/rotated_spectra/pallas_call | solution.py:147
  19.9 0.0 copy-start
  20.0 0.0 copy-start.4
  20.0 0.0 copy-start.10
  20.0 1.3 %collective-permute-done.2 = bf16[32,4224]{1,0:T(8,128)(2,1)S(1)} collective-permute-done((bf16[32,4224]{1,0:T(8,128)(2,1)S(1)}, bf16[32,4224]{1,0:T(8,128)(2,1)S(1)}, u32[]{:S(2)}, u32[]{:S(2)}) %collective-permute-start.2) | collective-permute-done | bytes 270368 | tf_op jit(solution)/shard_map/ppermute | solution.py:517
  21.3 0.0 copy-start.3
  21.3 0.0 copy-start.6
  21.3 0.0 copy-start.7
  21.4 0.1 collective-permute-start.3
  21.4 1.9 %collective-permute-done.3.far_ref = bf16[64,4224]{1,0:T(8,128)(2,1)S(1)} collective-permute-done((bf16[64,4224]{1,0:T(8,128)(2,1)S(1)}, bf16[64,4224]{1,0:T(8,128)(2,1)S(1)}, u32[]{:S(2)}, u32[]{:S(2)}) %collective-permute-start.3) | collective-permute-done | bytes 540704 | tf_op jit(solution)/shard_map/ppermute | solution.py:521
  23.4 0.0 copy-done.1
  23.4 0.0 copy-done.2
  23.4 0.0 copy-done
  23.4 0.0 copy-done.4
  23.4 0.0 copy-done.10
  23.4 16.1 %local_scores.1 = (bf16[1200,4096]{1,0:T(8,128)(2,1)S(1)}, f32[1200,256]{1,0:T(8,128)S(1)}, f32[16,1,8,128]{3,2,1,0:T(8,128)S(1)}) custom-call(s32[16]{0:T(128)S(1)} %copy-done.10, bf16[64,4224]{1,0:T(8,128)(2,1)S(1)} %pad_maximum_fusion.near_ref, bf16[64,4224]{1,0:T(8,128)(2,1)S(1)} %collective-permute-done.3.far_ref, bf16[96,4096]{1,0:T(8,128)(2,1)S(1)} %copy-done, ...), custom_call_target="tpu_custom_call" | custom-call | tf_op jit(solution)/shard_map/local_scores/pallas_call | solution.py:356
  39.5 13.3 %all_to_all.5.stats_ref = f32[16,1,8,128]{3,2,1,0:T(8,128)S(1)} all-to-all(f32[16,1,8,128]{3,2,1,0:T(8,128)S(1)} %get-tuple-element.11), channel_id=1, replica_groups=mesh['parts'=2,'blk'=16] {'blk'}, dimensions={0} | all-to-all | bytes 131072 | tf_op jit(solution)/shard_map/all_to_all | solution.py:527
  52.9 0.0 copy-done.3
  52.9 0.0 copy-done.6
  52.9 0.0 copy-done.7
  52.9 4.9 %local_sums.1 = (f32[1,8]{1,0:T(1,128)}, f32[4,2,2048]{2,1,0:T(2,128)}) custom-call(s32[16]{0:T(128)S(1)} %copy-done.10, f32[16,1,8,128]{3,2,1,0:T(8,128)S(1)} %all_to_all.5.stats_ref, f32[1200,256]{1,0:T(8,128)S(1)} %get-tuple-element.12.expo_ref, bf16[1200,4096]{1,0:T(8,128)(2,1)S(1)} %get-tuple-element.13.hat_ref, f32[64,256]{1,0:T(8,128)S(1)} %copy-done.7, ...), custom_call_target="tpu_custom_call" | custom-call | tf_op jit(solution)/shard_map/local_sums/pallas_call | solution.py:489
  (3 shorter events, 0.1 us)
Async XLA Ops:
  0.6 16.9 %copy-start.8 = (f32[64,128]{1,0:T(8,128)S(1)}, f32[64,128]{1,0:T(8,128)}, u32[]{:S(2)}) copy-start(f32[64,128]{1,0:T(8,128)} %constant.22.clone.sin_ref) | copy-start | bytes 98308
  0.6 16.9 %copy-start.9 = (f32[64,128]{1,0:T(8,128)S(1)}, f32[64,128]{1,0:T(8,128)}, u32[]{:S(2)}) copy-start(f32[64,128]{1,0:T(8,128)} %constant.21.clone.cos_ref) | copy-start | bytes 98308
  0.7 16.9 %copy-start.5 = (bf16[128,384]{1,0:T(8,128)(2,1)S(1)}, bf16[128,384]{1,0:T(8,128)(2,1)}, u32[]{:S(2)}) copy-start(bf16[128,384]{1,0:T(8,128)(2,1)} %constant.20.clone.trio_ref) | copy-start | bytes 294916
  0.7 16.9 %copy-start.11 = (f32[32]{0:T(128)S(1)}, f32[32]{0:T(128)}, u32[]{:S(2)}) copy-start(f32[32]{0:T(128)} %noise_ref.1) | copy-start | bytes 388
  1.8 7.8 %collective-permute-start = (bf16[8,4224]{1,0:T(8,128)(2,1)S(1)}, bf16[8,4224]{1,0:T(8,128)(2,1)S(1)}, u32[]{:S(2)}, u32[]{:S(2)}) collective-permute-start(bf16[8,4224]{1,0:T(8,128)(2,1)S(1)} %pack.1), channel_id=1, source_target_pairs={{0,8},{1,9},{2,10},{3,11},{4,12},{5,13},{6,14},{7,15},{8,0},{9,1},... | collective-permute-start | bytes 202760 | tf_op jit(solution)/shard_map/ppermute | solution.py:521
  9.6 5.1 %collective-permute-start.1 = (bf16[16,4224]{1,0:T(8,128)(2,1)S(1)}, bf16[16,4224]{1,0:T(8,128)(2,1)S(1)}, u32[]{:S(2)}, u32[]{:S(2)}) collective-permute-start(bf16[16,4224]{1,0:T(8,128)(2,1)S(1)} %pad_maximum_fusion.2), channel_id=1, source_target_pairs={{0,4},{1,5},{2,6},{3,7},{4,0},{5,1},{6,2},{7,3},{8,12},{9,13},{10,... | collective-permute-start | bytes 405512 | tf_op jit(solution)/shard_map/ppermute | solution.py:521
  14.7 6.5 %collective-permute-start.2 = (bf16[32,4224]{1,0:T(8,128)(2,1)S(1)}, bf16[32,4224]{1,0:T(8,128)(2,1)S(1)}, u32[]{:S(2)}, u32[]{:S(2)}) collective-permute-start(bf16[32,4224]{1,0:T(8,128)(2,1)S(1)} %pad_maximum_fusion.1), channel_id=1, source_target_pairs={{0,2},{1,3},{2,0},{3,1},{4,6},{5,7},{6,4},{7,5},{8,10},{9,11},{10,... | collective-permute-start | bytes 811016 | tf_op jit(solution)/shard_map/ppermute | solution.py:517
  17.6 5.8 %copy-start.1 = (f32[25,4096]{1,0:T(8,128)S(1)}, f32[25,4096]{1,0:T(8,128)}, u32[]{:S(2)}) copy-start(f32[25,4096]{1,0:T(8,128)} %constant.25.clone.ts_ref) | copy-start | bytes 1228804
  17.6 5.7 %copy-start.2 = (f32[25,4096]{1,0:T(8,128)S(1)}, f32[25,4096]{1,0:T(8,128)}, u32[]{:S(2)}) copy-start(f32[25,4096]{1,0:T(8,128)} %constant.24.clone.tc_ref) | copy-start | bytes 1228804
  19.9 3.4 %copy-start = (bf16[96,4096]{1,0:T(8,128)(2,1)S(1)}, bf16[96,4096]{1,0:T(8,128)(2,1)}, u32[]{:S(2)}) copy-start(bf16[96,4096]{1,0:T(8,128)(2,1)} %constant.23.clone.offset_ref) | copy-start | bytes 2359300
  20.0 3.4 %copy-start.4 = (bf16[256,256]{1,0:T(8,128)(2,1)S(1)}, bf16[256,256]{1,0:T(8,128)(2,1)}, u32[]{:S(2)}) copy-start(bf16[256,256]{1,0:T(8,128)(2,1)} %constant.26.clone.forward_ref) | copy-start | bytes 393220
  20.0 3.4 %copy-start.10 = (s32[16]{0:T(128)S(1)}, s32[16]{0:T(128)}, u32[]{:S(2)}) copy-start(s32[16]{0:T(128)} %counts_ref.3) | copy-start | bytes 196
  21.3 31.6 %copy-start.3 = (bf16[256,512]{1,0:T(8,128)(2,1)S(1)}, bf16[256,512]{1,0:T(8,128)(2,1)}, u32[]{:S(2)}) copy-start(bf16[256,512]{1,0:T(8,128)(2,1)} %constant.29.clone.image_ref) | copy-start | bytes 786436
  21.3 31.6 %copy-start.6 = (f32[64,256]{1,0:T(8,128)S(1)}, f32[64,256]{1,0:T(8,128)}, u32[]{:S(2)}) copy-start(f32[64,256]{1,0:T(8,128)} %constant.28.clone.sin_ref) | copy-start | bytes 196612
  21.3 31.5 %copy-start.7 = (f32[64,256]{1,0:T(8,128)S(1)}, f32[64,256]{1,0:T(8,128)}, u32[]{:S(2)}) copy-start(f32[64,256]{1,0:T(8,128)} %constant.27.clone.cos_ref) | copy-start | bytes 196612
  21.4 2.0 %collective-permute-start.3 = (bf16[64,4224]{1,0:T(8,128)(2,1)S(1)}, bf16[64,4224]{1,0:T(8,128)(2,1)S(1)}, u32[]{:S(2)}, u32[]{:S(2)}) collective-permute-start(bf16[64,4224]{1,0:T(8,128)(2,1)S(1)} %pad_maximum_fusion.near_ref), channel_id=1, source_target_pairs={{0,1},{1,0},{2,3},{3,2},{4,5},{5,4},{6,7},{7,6},{8,9},{9,8},{10,11... | collective-permute-start | bytes 1622024 | tf_op jit(solution)/shard_map/ppermute | solution.py:521

commit v4 on v3

--- a/solution.py
+++ b/solution.py
@@ -18,6 +18,7 @@
 PAIR = 4 * ANGLES
 WIDE = 16
 STEP_GROUPS = ((0, 1, 2, 3, 4, 5, 6, 7, 8), (9, 10, 11, 12))
+SCORE_STEPS = (9, 8, 8)
 F32 = jnp.float32
 BF16 = jnp.bfloat16
 MIB = 1024 * 1024
@@ -216,27 +217,51 @@
     lax.fori_loop(0, counts_ref.shape[0], add_start, jnp.int32(0))
 
 
-def score_chunk(
-    cycles, slots, chunk, counts_ref, near_ref, far_ref, offset_ref, tc_ref, ts_ref, forward_ref, bt_ref,
-    hat_ref, expo_ref, stats_ref, starts, plain_ref, swap_ref, stack_ref,
-):
+def choose(flip, slots, chunk, counts_ref, starts, ref):
     devices = counts_ref.shape[0]
     bits = devices.bit_length() - 1
     me = lax.axis_index("blk")
     width = devices // 2 * slots
     lane = lax.broadcasted_iota(jnp.int32, (1, width), 1)
     place = lane % slots
-    chosen = None
-    for flip, ref in ((0, near_ref), (1, far_ref)):
-        rank = jnp.full((1, width), -1, jnp.int32)
-        for k in range(devices // 2):
-            owner = me ^ (bit_reverse(k, bits) | flip)
-            here = (lane // slots == k) & (place < counts_ref[owner])
-            rank = jnp.where(here, starts[owner] + place, rank)
-        wanted = lax.broadcasted_iota(jnp.int32, (CHUNK, width), 0) + chunk * CHUNK
-        pick = (jnp.broadcast_to(rank, (CHUNK, width)) == wanted).astype(F32).astype(BF16)
-        term = dot(pick, ref[...])
-        chosen = term if chosen is None else chosen + term
+    rank = jnp.full((1, width), -1, jnp.int32)
+    for k in range(devices // 2):
+        owner = me ^ (bit_reverse(k, bits) | flip)
+        here = (lane // slots == k) & (place < counts_ref[owner])
+        rank = jnp.where(here, starts[owner] + place, rank)
+    wanted = lax.broadcasted_iota(jnp.int32, (CHUNK, width), 0) + chunk * CHUNK
+    pick = (jnp.broadcast_to(rank, (CHUNK, width)) == wanted).astype(F32).astype(BF16)
+    return dot(pick, ref[...])
+
+
+def near_kernel(slots, counts_ref, near_ref, out_ref, starts):
+    find_starts(counts_ref, starts)
+    out_ref[...] = choose(0, slots, 0, counts_ref, starts, near_ref)
+
+
+def near_choice(near, counts, slots):
+    vmem = pl.BlockSpec(memory_space=pltpu.VMEM)
+    return pl.pallas_call(
+        functools.partial(near_kernel, slots),
+        out_shape=pltpu.VMEM((CHUNK, near.shape[1]), F32),
+        in_specs=[pl.BlockSpec(memory_space=pltpu.SMEM), vmem],
+        out_specs=vmem,
+        scratch_shapes=[pltpu.SMEM(counts.shape, jnp.int32)],
+        compiler_params=pltpu.CompilerParams(vmem_limit_bytes=8 * MIB),
+        cost_estimate=pl.CostEstimate(flops=10**9, bytes_accessed=10**6, transcendentals=0),
+        name="near_choice",
+    )(counts, pltpu.with_memory_space_constraint(near, pltpu.VMEM))
+
+
+def score_chunk(
+    cycles, slots, chunk, counts_ref, near_ref, far_ref, offset_ref, tc_ref, ts_ref, forward_ref, bt_ref,
+    hat_ref, expo_ref, stats_ref, starts, plain_ref, swap_ref, stack_ref,
+):
+    if near_ref.dtype == F32:
+        chosen = near_ref[...]
+    else:
+        chosen = choose(0, slots, chunk, counts_ref, starts, near_ref)
+    chosen = chosen + choose(1, slots, chunk, counts_ref, starts, far_ref)
 
     span = cycles * ANGLES
     offset_x = chosen[:, 2 * span : 2 * span + 1]
@@ -292,8 +317,12 @@
     lax.fori_loop(0, cycles // 2, transform, 0)
 
     columns = expo_ref.shape[1]
-    both = dot(hat_ref[...], bt_ref[...], ((1,), (1,)))
-    expo_ref[...] = both[:, :columns] + both[:, columns:]
+    at = 0
+    for steps in SCORE_STEPS:
+        rows = slice(at * CHUNK, (at + steps) * CHUNK)
+        both = dot(hat_ref[rows, :], bt_ref[...], ((1,), (1,)))
+        expo_ref[rows, :] = both[:, :columns] + both[:, columns:]
+        at += steps
     step_rows = [slice(t * CHUNK, (t + 1) * CHUNK) for t in range(STEPS)]
     top = expo_ref[step_rows[0], :]
     for rows in step_rows[1:]:
@@ -312,7 +341,7 @@
     mass_row = jnp.sum(jnp.where(diagonal, mass, 0.0), axis=0, keepdims=True)
     which = lax.broadcasted_iota(jnp.int32, (8, 128), 0)
     tile = jnp.where(which == 0, peak_row, jnp.where(which == 1, mass_row, 0.0))
-    for d in range(devices):
+    for d in range(stats_ref.shape[0]):
         stats_ref[d, chunk] = tile
 
 
@@ -523,7 +552,12 @@
             break
         packed = jnp.concatenate([packed, moved], axis=0)
         distance //= 2
-    hat, expo, stats = local_scores(packed, moved, counts, spectra, cycles, slots, chunks)
+    near = packed
+    if chunks == 1:
+        near = near_choice(packed, counts, slots)
+        moved, near = lax.optimization_barrier((moved, near))
+        near = pltpu.with_memory_space_constraint(near, pltpu.VMEM)
+    hat, expo, stats = local_scores(near, moved, counts, spectra, cycles, slots, chunks)
     stats = lax.all_to_all(stats, "blk", 0, 0, tiled=True)
     loglik, class_sums = local_sums(counts, stats, expo, hat, classes, cycles, slots, chunks)
     return (loglik.reshape(slots), class_sums)

time: 58 us -> 57.8 us (level)
  waiting for transfers between devices: 11.3 us -> 10.4 us
  Pallas kernels: 24.4 us -> 25.1 us
    ppermute x4, waiting for transfers between devices: 11.3 us -> 10.4 us  [local(): lax.ppermute(packed, 'blk', [(i, i ^ distance) for i in range(devices)])]
    pallas_call x0 -> x1, Pallas kernels: none -> 0.9 us  [near_choice(): pl.pallas_call(functools.partial(near_kernel, slots), out_shape=pltpu.VME...]
  transfers between devices with their start and end apart: 4 -> 4, of which waited for: 4 -> 4; matrix products, arithmetic and copies ran while one was open for 2% -> 2% of each run, Pallas kernels for 4% -> 6%
where the time goes in v4:
time: 57.8 us; the launch traced here: 57.5 us
  Pallas kernels  25.1 us (43%)
  blocking collectives  13.3 us (23%)
  waiting for transfers between devices  10.4 us (18%)
  starting transfers between devices  6.62 us (11%)
  local copies, waits for them, and re-layouts  1.1 us (2%)
  between operations  0.83 us (1%)
    pallas_call x1, Pallas kernels, local_scores(): pl.pallas_call(functools.partial(score_kernel, cycles, slots, chunks), ou...  16 us
    all_to_all x1, blocking collectives, local(): stats = lax.all_to_all(stats, 'blk', 0, 0, tiled=True)  13.3 us
    ppermute x4, waiting for transfers between devices, local(): lax.ppermute(packed, 'blk', [(i, i ^ distance) for i in range(devices)])  10.4 us
    ppermute x4, starting transfers between devices, local(): lax.ppermute(packed, 'blk', [(i, i ^ distance) for i in range(devices)])  6.62 us
    pallas_call x1, Pallas kernels, local_sums(): pl.pallas_call(functools.partial(sum_kernel, classes, chunks), out_shape=...  4.86 us
    pallas_call x1, Pallas kernels, rotated_spectra(): pl.pallas_call(functools.partial(spectra_kernel, cycles), out_shape=pltpu...  2.31 us
  transfers between devices with their start and end apart: 4, of which 4 were waited for; matrix products, arithmetic and copies ran while one was open for 2% of the time, Pallas kernels for 6%

profile of v4, /device:TPU:0, one launch (start us, length us, event | category | flops | bytes accessed | tf_op | source)
XLA Modules:
  0.0 57.5 jit_solution(17499286153744999172)
XLA Ops:
  0.6 0.0 copy-start.8
  0.6 0.0 copy-start.9
  0.7 0.0 copy-start.5
  0.7 0.0 copy-start.11
  0.7 1.1 %pack.1 = bf16[8,4224]{1,0:T(8,128)(2,1)S(1)} custom-call(bf16[8,2,2048]{2,1,0:T(2,128)(2,1)} %particles_hbm.1, s32[2,8]{1,0:T(2,128)} %offsets_hbm.1), custom_call_target="tpu_custom_call" | custom-call | tf_op jit(solution)/shard_map/pack/pallas_call | solution.py:194
  1.8 4.1 %collective-permute-start = (bf16[8,4224]{1,0:T(8,128)(2,1)S(1)}, bf16[8,4224]{1,0:T(8,128)(2,1)S(1)}, u32[]{:S(2)}, u32[]{:S(2)}) collective-permute-start(bf16[8,4224]{1,0:T(8,128)(2,1)S(1)} %pack.1), channel_id=1, source_target_pairs={{0,8},{1,9},{2,10},{3,11},{4,12},{5,13},{6,14},{7,15},{8,0},{9,1},... | collective-permute-start | bytes 202760 | tf_op jit(solution)/shard_map/ppermute | solution.py:550
  5.9 3.7 %collective-permute-done = bf16[8,4224]{1,0:T(8,128)(2,1)S(1)} collective-permute-done((bf16[8,4224]{1,0:T(8,128)(2,1)S(1)}, bf16[8,4224]{1,0:T(8,128)(2,1)S(1)}, u32[]{:S(2)}, u32[]{:S(2)}) %collective-permute-start) | collective-permute-done | bytes 67616 | tf_op jit(solution)/shard_map/ppermute | solution.py:550
  9.6 0.7 %collective-permute-start.1 = (bf16[16,4224]{1,0:T(8,128)(2,1)S(1)}, bf16[16,4224]{1,0:T(8,128)(2,1)S(1)}, u32[]{:S(2)}, u32[]{:S(2)}) collective-permute-start(bf16[16,4224]{1,0:T(8,128)(2,1)S(1)} %pad_maximum_fusion.2), channel_id=1, source_target_pairs={{0,4},{1,5},{2,6},{3,7},{4,0},{5,1},{6,2},{7,3},{8,12},{9,13},{10,... | collective-permute-start | bytes 405512 | tf_op jit(solution)/shard_map/ppermute | solution.py:550
  10.3 4.4 %collective-permute-done.1 = bf16[16,4224]{1,0:T(8,128)(2,1)S(1)} collective-permute-done((bf16[16,4224]{1,0:T(8,128)(2,1)S(1)}, bf16[16,4224]{1,0:T(8,128)(2,1)S(1)}, u32[]{:S(2)}, u32[]{:S(2)}) %collective-permute-start.1) | collective-permute-done | bytes 135200 | tf_op jit(solution)/shard_map/ppermute | solution.py:550
  14.7 1.8 %collective-permute-start.2 = (bf16[32,4224]{1,0:T(8,128)(2,1)S(1)}, bf16[32,4224]{1,0:T(8,128)(2,1)S(1)}, u32[]{:S(2)}, u32[]{:S(2)}) collective-permute-start(bf16[32,4224]{1,0:T(8,128)(2,1)S(1)} %pad_maximum_fusion.1), channel_id=1, source_target_pairs={{0,2},{1,3},{2,0},{3,1},{4,6},{5,7},{6,4},{7,5},{8,10},{9,11},{10,... | collective-permute-start | bytes 811016 | tf_op jit(solution)/shard_map/ppermute | solution.py:546
  16.5 0.9 %reshape.13 = bf16[4,2,32,64]{3,2,1,0:T(8,128)(2,1)S(1)} reshape(bf16[4,2,2048]{2,1,0:T(2,128)(2,1)} %param.17) | data formatting | bytes 65536 | tf_op jit(solution)/shard_map/reshape | solution.py:142
  17.4 0.1 copy.19
  17.5 0.1 reshape.14.refs_ref
  17.6 0.0 copy-done.8
  17.6 0.0 copy-done.9
  17.6 0.0 copy-done.5
  17.6 0.0 copy-done.11
  17.6 0.0 copy-start.10
  17.6 2.3 %rotated_spectra.1.bt_ref = bf16[512,4096]{1,0:T(8,128)(2,1)S(1)} custom-call(f32[32]{0:T(128)S(1)} %copy-done.11, bf16[128,128]{1,0:T(8,128)(2,1)S(1)} %reshape.14.refs_ref, bf16[128,384]{1,0:T(8,128)(2,1)S(1)} %copy-done.5, f32[64,128]{1,0:T(8,128)S(1)} %copy-done.9, f32[64,128]{1,0:T(8,128)S(1)} %copy-done.8), custom_call_target="tpu_custom_call" | custom-call | flops 16777216 | bytes 4194304 | tf_op jit(solution)/shard_map/rotated_spectra/pallas_call | solution.py:148
  19.9 1.3 %collective-permute-done.2 = bf16[32,4224]{1,0:T(8,128)(2,1)S(1)} collective-permute-done((bf16[32,4224]{1,0:T(8,128)(2,1)S(1)}, bf16[32,4224]{1,0:T(8,128)(2,1)S(1)}, u32[]{:S(2)}, u32[]{:S(2)}) %collective-permute-start.2) | collective-permute-done | bytes 270368 | tf_op jit(solution)/shard_map/ppermute | solution.py:546
  21.3 0.0 copy-start
  21.3 0.0 copy-start.1
  21.3 0.0 copy-start.2
  21.4 0.0 copy-start.4
  21.4 0.1 collective-permute-start.3
  21.4 0.0 copy-done.10
  21.5 0.9 %near_choice.1.near_ref = f32[48,4224]{1,0:T(8,128)S(1)} custom-call(s32[16]{0:T(128)S(1)} %copy-done.10, bf16[64,4224]{1,0:T(8,128)(2,1)S(1)} %pad_maximum_fusion.near_ref), custom_call_target="tpu_custom_call" | custom-call | flops 1000000000 | bytes 1000000 | tf_op jit(solution)/shard_map/near_choice/pallas_call | solution.py:244
  22.4 0.0 copy-start.3
  22.4 0.0 copy-start.6
  22.4 0.0 copy-start.7
  22.4 1.0 %collective-permute-done.3.far_ref = bf16[64,4224]{1,0:T(8,128)(2,1)S(1)} collective-permute-done((bf16[64,4224]{1,0:T(8,128)(2,1)S(1)}, bf16[64,4224]{1,0:T(8,128)(2,1)S(1)}, u32[]{:S(2)}, u32[]{:S(2)}) %collective-permute-start.3) | collective-permute-done | bytes 540704 | tf_op jit(solution)/shard_map/ppermute | solution.py:550
  23.4 0.0 copy-done
  23.4 0.0 copy-done.1
  23.4 0.0 copy-done.2
  23.4 0.0 copy-done.4
  23.4 16.0 %local_scores.1 = (bf16[1200,4096]{1,0:T(8,128)(2,1)S(1)}, f32[1200,256]{1,0:T(8,128)S(1)}, f32[16,1,8,128]{3,2,1,0:T(8,128)S(1)}) custom-call(s32[16]{0:T(128)S(1)} %copy-done.10, f32[48,4224]{1,0:T(8,128)S(1)} %near_choice.1.near_ref, bf16[64,4224]{1,0:T(8,128)(2,1)S(1)} %collective-permute-done.3.far_ref, bf16[96,4096]{1,0:T(8,128)(2,1)S(1)} %copy-done, ...), custom_call_target="tpu_custom_call" | custom-call | tf_op jit(solution)/shard_map/local_scores/pallas_call | solution.py:385
  39.3 13.3 %all_to_all.5.stats_ref = f32[16,1,8,128]{3,2,1,0:T(8,128)S(1)} all-to-all(f32[16,1,8,128]{3,2,1,0:T(8,128)S(1)} %get-tuple-element.15), channel_id=1, replica_groups=mesh['parts'=2,'blk'=16] {'blk'}, dimensions={0} | all-to-all | bytes 131072 | tf_op jit(solution)/shard_map/all_to_all | solution.py:561
  52.7 0.0 copy-done.3
  52.7 0.0 copy-done.6
  52.7 0.0 copy-done.7
  52.7 4.9 %local_sums.1 = (f32[1,8]{1,0:T(1,128)}, f32[4,2,2048]{2,1,0:T(2,128)}) custom-call(s32[16]{0:T(128)S(1)} %copy-done.10, f32[16,1,8,128]{3,2,1,0:T(8,128)S(1)} %all_to_all.5.stats_ref, f32[1200,256]{1,0:T(8,128)S(1)} %get-tuple-element.16.expo_ref, bf16[1200,4096]{1,0:T(8,128)(2,1)S(1)} %get-tuple-element.17.hat_ref, f32[64,256]{1,0:T(8,128)S(1)} %copy-done.7, ...), custom_call_target="tpu_custom_call" | custom-call | tf_op jit(solution)/shard_map/local_sums/pallas_call | solution.py:518
  (3 shorter events, 0.1 us)
Async XLA Ops:
  0.6 16.9 %copy-start.8 = (f32[64,128]{1,0:T(8,128)S(1)}, f32[64,128]{1,0:T(8,128)}, u32[]{:S(2)}) copy-start(f32[64,128]{1,0:T(8,128)} %constant.22.clone.sin_ref) | copy-start | bytes 98308
  0.6 16.9 %copy-start.9 = (f32[64,128]{1,0:T(8,128)S(1)}, f32[64,128]{1,0:T(8,128)}, u32[]{:S(2)}) copy-start(f32[64,128]{1,0:T(8,128)} %constant.21.clone.cos_ref) | copy-start | bytes 98308
  0.7 16.9 %copy-start.5 = (bf16[128,384]{1,0:T(8,128)(2,1)S(1)}, bf16[128,384]{1,0:T(8,128)(2,1)}, u32[]{:S(2)}) copy-start(bf16[128,384]{1,0:T(8,128)(2,1)} %constant.20.clone.trio_ref) | copy-start | bytes 294916
  0.7 16.9 %copy-start.11 = (f32[32]{0:T(128)S(1)}, f32[32]{0:T(128)}, u32[]{:S(2)}) copy-start(f32[32]{0:T(128)} %noise_ref.1) | copy-start | bytes 388
  1.8 7.8 %collective-permute-start = (bf16[8,4224]{1,0:T(8,128)(2,1)S(1)}, bf16[8,4224]{1,0:T(8,128)(2,1)S(1)}, u32[]{:S(2)}, u32[]{:S(2)}) collective-permute-start(bf16[8,4224]{1,0:T(8,128)(2,1)S(1)} %pack.1), channel_id=1, source_target_pairs={{0,8},{1,9},{2,10},{3,11},{4,12},{5,13},{6,14},{7,15},{8,0},{9,1},... | collective-permute-start | bytes 202760 | tf_op jit(solution)/shard_map/ppermute | solution.py:550
  9.6 5.1 %collective-permute-start.1 = (bf16[16,4224]{1,0:T(8,128)(2,1)S(1)}, bf16[16,4224]{1,0:T(8,128)(2,1)S(1)}, u32[]{:S(2)}, u32[]{:S(2)}) collective-permute-start(bf16[16,4224]{1,0:T(8,128)(2,1)S(1)} %pad_maximum_fusion.2), channel_id=1, source_target_pairs={{0,4},{1,5},{2,6},{3,7},{4,0},{5,1},{6,2},{7,3},{8,12},{9,13},{10,... | collective-permute-start | bytes 405512 | tf_op jit(solution)/shard_map/ppermute | solution.py:550
  14.7 6.5 %collective-permute-start.2 = (bf16[32,4224]{1,0:T(8,128)(2,1)S(1)}, bf16[32,4224]{1,0:T(8,128)(2,1)S(1)}, u32[]{:S(2)}, u32[]{:S(2)}) collective-permute-start(bf16[32,4224]{1,0:T(8,128)(2,1)S(1)} %pad_maximum_fusion.1), channel_id=1, source_target_pairs={{0,2},{1,3},{2,0},{3,1},{4,6},{5,7},{6,4},{7,5},{8,10},{9,11},{10,... | collective-permute-start | bytes 811016 | tf_op jit(solution)/shard_map/ppermute | solution.py:546
  17.6 3.8 %copy-start.10 = (s32[16]{0:T(128)S(1)}, s32[16]{0:T(128)}, u32[]{:S(2)}) copy-start(s32[16]{0:T(128)} %counts_ref.5) | copy-start | bytes 196
  21.3 2.1 %copy-start = (bf16[96,4096]{1,0:T(8,128)(2,1)S(1)}, bf16[96,4096]{1,0:T(8,128)(2,1)}, u32[]{:S(2)}) copy-start(bf16[96,4096]{1,0:T(8,128)(2,1)} %constant.23.clone.offset_ref) | copy-start | bytes 2359300
  21.3 2.0 %copy-start.1 = (f32[25,4096]{1,0:T(8,128)S(1)}, f32[25,4096]{1,0:T(8,128)}, u32[]{:S(2)}) copy-start(f32[25,4096]{1,0:T(8,128)} %constant.25.clone.ts_ref) | copy-start | bytes 1228804
  21.3 2.0 %copy-start.2 = (f32[25,4096]{1,0:T(8,128)S(1)}, f32[25,4096]{1,0:T(8,128)}, u32[]{:S(2)}) copy-start(f32[25,4096]{1,0:T(8,128)} %constant.24.clone.tc_ref) | copy-start | bytes 1228804
  21.4 2.0 %copy-start.4 = (bf16[256,256]{1,0:T(8,128)(2,1)S(1)}, bf16[256,256]{1,0:T(8,128)(2,1)}, u32[]{:S(2)}) copy-start(bf16[256,256]{1,0:T(8,128)(2,1)} %constant.26.clone.forward_ref) | copy-start | bytes 393220
  21.4 2.0 %collective-permute-start.3 = (bf16[64,4224]{1,0:T(8,128)(2,1)S(1)}, bf16[64,4224]{1,0:T(8,128)(2,1)S(1)}, u32[]{:S(2)}, u32[]{:S(2)}) collective-permute-start(bf16[64,4224]{1,0:T(8,128)(2,1)S(1)} %pad_maximum_fusion.near_ref), channel_id=1, source_target_pairs={{0,1},{1,0},{2,3},{3,2},{4,5},{5,4},{6,7},{7,6},{8,9},{9,8},{10,11... | collective-permute-start | bytes 1622024 | tf_op jit(solution)/shard_map/ppermute | solution.py:550
  22.4 30.3 %copy-start.3 = (bf16[256,512]{1,0:T(8,128)(2,1)S(1)}, bf16[256,512]{1,0:T(8,128)(2,1)}, u32[]{:S(2)}) copy-start(bf16[256,512]{1,0:T(8,128)(2,1)} %constant.29.clone.image_ref) | copy-start | bytes 786436
  22.4 30.3 %copy-start.6 = (f32[64,256]{1,0:T(8,128)S(1)}, f32[64,256]{1,0:T(8,128)}, u32[]{:S(2)}) copy-start(f32[64,256]{1,0:T(8,128)} %constant.28.clone.sin_ref) | copy-start | bytes 196612
  22.4 30.3 %copy-start.7 = (f32[64,256]{1,0:T(8,128)S(1)}, f32[64,256]{1,0:T(8,128)}, u32[]{:S(2)}) copy-start(f32[64,256]{1,0:T(8,128)} %constant.27.clone.cos_ref) | copy-start | bytes 196612
